TPU v7x, 32 devices: a whole 2x2x4 slice. The times are simulated.
32 devices in a mesh: wide: 4 (over z), narrow: 8 (over y, x, core).
Axes of the slice: x: 2, y: 2, z: 4, core: 2. Of those that a mesh axis runs over, the one named last changes fastest.
Arguments:
- acts: bfloat16 [32, 128, 2048], P(('wide', 'narrow')), parts along dimension 0, may hold values from -6 to 6
- cotangent: bfloat16 [32, 128, 2048], P(('wide', 'narrow')), parts along dimension 0, may hold values from -0.5 to 0.5
- down_matrix: bfloat16 [64, 2048], replicated, may hold values from -0.125 to 0.125
- up_matrix: bfloat16 [2048, 64], replicated, may hold values from -0.125 to 0.125
- adam_first_moment: float32 [262144], P('narrow'), may hold values from -0.6 to 0.6
- adam_second_moment: float32 [262144], P('narrow'), may hold values from 0.05 to 5
- lengths: int32 [32], P(('wide', 'narrow')), parts along dimension 0, may hold values from 32 to 128, as said below
- sign_hash_salt: int32 [1], replicated, may hold values from 0 to 999999
Outputs:
- features: float32 [32, 4096], P(('wide', 'narrow')), parts along dimension 0
There are 4 independent parts, one for each index of `wide`. A program takes and returns all parts, laid end to end along the dimension named above; an argument that names none is the same for every part. Nothing has to cross between parts.
Inputs may be any that keep to these rules, and one draw needn't show every extreme that they name: `lengths`: tokens at or after a sequence's length are padding. Some sequence of each batch has exactly 128 and another exactly 32.
All inputs are finite; a program needn't handle non-finite values.
Results may differ from a plain program's by a relative error of at most 0.0033.
Values may be sent and summed in bfloat16 or wider, within the bound.
No kernel may reach another device: no remote copies, remote signals or barrier semaphores. Data moves between devices by JAX's collectives and lax.ppermute only.
A program may use at most 64 MiB of HBM per device.

v0:
```python
import math

import jax
import jax.numpy as jnp
from jax import lax
from jax.sharding import PartitionSpec as P

FEAT = 4096
BLOCKS = 4
PARAMS = 262144


def rademacher(row_start, rows, col_start, cols, sign_hash_salt):
    row = lax.broadcasted_iota(jnp.int32, (rows, cols), 0) + row_start
    col = lax.broadcasted_iota(jnp.int32, (rows, cols), 1) + col_start
    mixed = row * FEAT + col ^ sign_hash_salt[0]
    mixed = mixed * 747796405 + 1
    mixed = mixed ^ mixed >> 15
    mixed = mixed * 277803737
    mixed = mixed ^ mixed >> 13
    return (1 - 2 * (mixed >> 7 & 1)).astype(jnp.bfloat16)


def adam_scale(grads, adam_first_moment, adam_second_moment):
    moment_one = 0.9 * adam_first_moment[None, :] + 0.1 * grads
    moment_two = 0.999 * adam_second_moment[None, :] + 0.001 * grads * grads
    return (moment_one / (jnp.sqrt(moment_two) + 1e-08)).astype(jnp.bfloat16)


def project_rows(updates, first_row, col_start, width, sign_hash_salt):
    share = updates.shape[1]
    step_rows = math.gcd(share, 2048)

    def add_block(index, total):
        start = index * step_rows
        rows = lax.dynamic_slice_in_dim(updates, start, step_rows, 1)
        signs = rademacher(first_row + start, step_rows, col_start, width, sign_hash_salt)
        return total + jnp.dot(rows, signs, preferred_element_type=jnp.float32)

    empty = jnp.zeros((updates.shape[0], width), jnp.float32)
    return lax.fori_loop(0, share // step_rows, add_block, empty)


def body(
    acts,
    cotangent,
    down_matrix,
    up_matrix,
    adam_first_moment,
    adam_second_moment,
    lengths,
    sign_hash_salt,
):
    local_seqs = acts.shape[0]
    positions = jnp.arange(acts.shape[1], dtype=jnp.int32)
    mask = (positions[None, :] < lengths[:, None]).astype(jnp.bfloat16)
    masked_tokens = cotangent * mask[:, :, None]
    hidden_state = jnp.einsum(
        "tyn,jn->tyj", acts, down_matrix, preferred_element_type=jnp.float32
    ).astype(jnp.bfloat16)
    inner_product = jnp.einsum(
        "ofy,yj->ofj", masked_tokens, up_matrix, preferred_element_type=jnp.float32
    ).astype(jnp.bfloat16)
    down_gradient = jnp.einsum(
        "uwj,uwi->uji", inner_product, acts, preferred_element_type=jnp.float32
    )
    up_gradient = jnp.einsum(
        "uwj,uwi->uji", hidden_state, masked_tokens, preferred_element_type=jnp.float32
    )
    grads = jnp.concatenate([down_gradient, up_gradient], axis=1).reshape(local_seqs, PARAMS)
    width = FEAT // BLOCKS
    regrouped = lax.all_to_all(grads, "narrow", split_axis=1, concat_axis=0, tiled=True)
    updates = adam_scale(regrouped, adam_first_moment, adam_second_moment)
    share = updates.shape[1]
    first_row = lax.axis_index("narrow") * share
    pieces = []
    for column in range(BLOCKS):
        term = project_rows(updates, first_row, column * width, width, sign_hash_salt)
        pieces.append(term)
    summed = lax.psum_scatter(
        jnp.concatenate(pieces, axis=1), "narrow", scatter_dimension=0, tiled=True
    )
    return summed * PARAMS ** (-0.5)


def solution(mesh):
    placed = (
        P(("wide", "narrow"), None, None),
        P(("wide", "narrow"), None, None),
        P(),
        P(),
        P("narrow"),
        P("narrow"),
        P(("wide", "narrow")),
        P(),
    )
    return jax.shard_map(
        body, mesh=mesh, in_specs=placed, out_specs=P(("wide", "narrow"), None), check_vma=False
    )
```

profile of v0, /device:TPU:0, one launch (start us, length us, event | category | flops | bytes accessed | tf_op | source)
XLA Modules:
  0.0 404.4 jit_solution(2746419032610121621)
XLA Ops:
  12.4 5.3 %all-to-all-start = ((f32[1,8,32768]{2,0,1:T(1,128)}), f32[1,8,32768]{2,0,1:T(1,128)S(1)}, u32[]{:S(2)}, u32[]{:S(2)}) async-start(f32[1,8,32768]{2,0,1:T(1,128)} %all_to_all.15), calls=%async_computation | async-start | bytes 2097152 | tf_op jit(solution)/shard_map/all_to_all | solution.py:72
  18.1 15.1 %all-to-all-done = f32[1,8,32768]{2,0,1:T(1,128)S(1)} async-done(((f32[1,8,32768]{2,0,1:T(1,128)}), f32[1,8,32768]{2,0,1:T(1,128)S(1)}, u32[]{:S(2)}, u32[]{:S(2)}) %all-to-all-start) | async-done | bytes 1048608 | tf_op jit(solution)/shard_map/all_to_all | solution.py:72
  34.0 78.8 %while.56 = (s32[]{:T(128)}, f32[8,1024]{1,0:T(8,128)S(1)}, bf16[8,32768]{1,0:T(8,128)(2,1)S(1)}, s32[]{:T(128)}, s32[1]{0:T(128)}, /*index=5*/s32[]{:T(128)}, s32[]{:T(128)}, s32[]{:T(128)}, s32[]{:T(128)}) while((s32[]{:T(128)}, f32[8,1024]{1,0:T(8,128)S(1)}, bf16[8,32768]{1,0:T(8,128)(2,1)S(1)}, s32[]{:T(128)}, s32[1]{0:T(128)}, ...), condition=%wide.region_1.0_spmd.clone, body=%wide.region_0.0_spmd.clone.sunk | while | flops 62935048 | bytes 114861 | solution.py:41
  34.0 4.9 %fusion.114 = f32[8,1024]{1,0:T(8,128)S(1)} fusion(s32[]{:T(128)} %bitcast.37, s32[2048]{0:T(1024)S(1)} %add_multiply_fusion.8, f32[8,1024]{1,0:T(8,128)S(1)} %get-tuple-element.714, bf16[8,32768]{1,0:T(8,128)(2,1)S(1)} %get-tuple-element.724, s32[]{:T(128)S(6)} %select_n.36, pred[]{:T(512)S(6)} %compare.12), kind=kOutput, calls=%fused_computation.9.clone.1 | convolution fusion | flops 62930944 | bytes 106505 | tf_op jit(solution)/shard_map/while/body/eval_jaxpr/dot_general | solution.py:38
  39.0 4.9 %fusion.114 = f32[8,1024]{1,0:T(8,128)S(1)} fusion(s32[]{:T(128)} %bitcast.37, s32[2048]{0:T(1024)S(1)} %add_multiply_fusion.8, f32[8,1024]{1,0:T(8,128)S(1)} %get-tuple-element.714, bf16[8,32768]{1,0:T(8,128)(2,1)S(1)} %get-tuple-element.724, s32[]{:T(128)S(6)} %select_n.36, pred[]{:T(512)S(6)} %compare.12), kind=kOutput, calls=%fused_computation.9.clone.1 | convolution fusion | flops 62930944 | bytes 106505 | tf_op jit(solution)/shard_map/while/body/eval_jaxpr/dot_general | solution.py:38
  43.9 4.9 %fusion.114 = f32[8,1024]{1,0:T(8,128)S(1)} fusion(s32[]{:T(128)} %bitcast.37, s32[2048]{0:T(1024)S(1)} %add_multiply_fusion.8, f32[8,1024]{1,0:T(8,128)S(1)} %get-tuple-element.714, bf16[8,32768]{1,0:T(8,128)(2,1)S(1)} %get-tuple-element.724, s32[]{:T(128)S(6)} %select_n.36, pred[]{:T(512)S(6)} %compare.12), kind=kOutput, calls=%fused_computation.9.clone.1 | convolution fusion | flops 62930944 | bytes 106505 | tf_op jit(solution)/shard_map/while/body/eval_jaxpr/dot_general | solution.py:38
  48.8 4.9 %fusion.114 = f32[8,1024]{1,0:T(8,128)S(1)} fusion(s32[]{:T(128)} %bitcast.37, s32[2048]{0:T(1024)S(1)} %add_multiply_fusion.8, f32[8,1024]{1,0:T(8,128)S(1)} %get-tuple-element.714, bf16[8,32768]{1,0:T(8,128)(2,1)S(1)} %get-tuple-element.724, s32[]{:T(128)S(6)} %select_n.36, pred[]{:T(512)S(6)} %compare.12), kind=kOutput, calls=%fused_computation.9.clone.1 | convolution fusion | flops 62930944 | bytes 106505 | tf_op jit(solution)/shard_map/while/body/eval_jaxpr/dot_general | solution.py:38
  53.7 4.9 %fusion.114 = f32[8,1024]{1,0:T(8,128)S(1)} fusion(s32[]{:T(128)} %bitcast.37, s32[2048]{0:T(1024)S(1)} %add_multiply_fusion.8, f32[8,1024]{1,0:T(8,128)S(1)} %get-tuple-element.714, bf16[8,32768]{1,0:T(8,128)(2,1)S(1)} %get-tuple-element.724, s32[]{:T(128)S(6)} %select_n.36, pred[]{:T(512)S(6)} %compare.12), kind=kOutput, calls=%fused_computation.9.clone.1 | convolution fusion | flops 62930944 | bytes 106505 | tf_op jit(solution)/shard_map/while/body/eval_jaxpr/dot_general | solution.py:38
  58.7 4.9 %fusion.114 = f32[8,1024]{1,0:T(8,128)S(1)} fusion(s32[]{:T(128)} %bitcast.37, s32[2048]{0:T(1024)S(1)} %add_multiply_fusion.8, f32[8,1024]{1,0:T(8,128)S(1)} %get-tuple-element.714, bf16[8,32768]{1,0:T(8,128)(2,1)S(1)} %get-tuple-element.724, s32[]{:T(128)S(6)} %select_n.36, pred[]{:T(512)S(6)} %compare.12), kind=kOutput, calls=%fused_computation.9.clone.1 | convolution fusion | flops 62930944 | bytes 106505 | tf_op jit(solution)/shard_map/while/body/eval_jaxpr/dot_general | solution.py:38
  63.6 4.9 %fusion.114 = f32[8,1024]{1,0:T(8,128)S(1)} fusion(s32[]{:T(128)} %bitcast.37, s32[2048]{0:T(1024)S(1)} %add_multiply_fusion.8, f32[8,1024]{1,0:T(8,128)S(1)} %get-tuple-element.714, bf16[8,32768]{1,0:T(8,128)(2,1)S(1)} %get-tuple-element.724, s32[]{:T(128)S(6)} %select_n.36, pred[]{:T(512)S(6)} %compare.12), kind=kOutput, calls=%fused_computation.9.clone.1 | convolution fusion | flops 62930944 | bytes 106505 | tf_op jit(solution)/shard_map/while/body/eval_jaxpr/dot_general | solution.py:38
  68.5 4.9 %fusion.114 = f32[8,1024]{1,0:T(8,128)S(1)} fusion(s32[]{:T(128)} %bitcast.37, s32[2048]{0:T(1024)S(1)} %add_multiply_fusion.8, f32[8,1024]{1,0:T(8,128)S(1)} %get-tuple-element.714, bf16[8,32768]{1,0:T(8,128)(2,1)S(1)} %get-tuple-element.724, s32[]{:T(128)S(6)} %select_n.36, pred[]{:T(512)S(6)} %compare.12), kind=kOutput, calls=%fused_computation.9.clone.1 | convolution fusion | flops 62930944 | bytes 106505 | tf_op jit(solution)/shard_map/while/body/eval_jaxpr/dot_general | solution.py:38
  73.4 4.9 %fusion.114 = f32[8,1024]{1,0:T(8,128)S(1)} fusion(s32[]{:T(128)} %bitcast.37, s32[2048]{0:T(1024)S(1)} %add_multiply_fusion.8, f32[8,1024]{1,0:T(8,128)S(1)} %get-tuple-element.714, bf16[8,32768]{1,0:T(8,128)(2,1)S(1)} %get-tuple-element.724, s32[]{:T(128)S(6)} %select_n.36, pred[]{:T(512)S(6)} %compare.12), kind=kOutput, calls=%fused_computation.9.clone.1 | convolution fusion | flops 62930944 | bytes 106505 | tf_op jit(solution)/shard_map/while/body/eval_jaxpr/dot_general | solution.py:38
  78.4 4.9 %fusion.114 = f32[8,1024]{1,0:T(8,128)S(1)} fusion(s32[]{:T(128)} %bitcast.37, s32[2048]{0:T(1024)S(1)} %add_multiply_fusion.8, f32[8,1024]{1,0:T(8,128)S(1)} %get-tuple-element.714, bf16[8,32768]{1,0:T(8,128)(2,1)S(1)} %get-tuple-element.724, s32[]{:T(128)S(6)} %select_n.36, pred[]{:T(512)S(6)} %compare.12), kind=kOutput, calls=%fused_computation.9.clone.1 | convolution fusion | flops 62930944 | bytes 106505 | tf_op jit(solution)/shard_map/while/body/eval_jaxpr/dot_general | solution.py:38
  83.3 4.9 %fusion.114 = f32[8,1024]{1,0:T(8,128)S(1)} fusion(s32[]{:T(128)} %bitcast.37, s32[2048]{0:T(1024)S(1)} %add_multiply_fusion.8, f32[8,1024]{1,0:T(8,128)S(1)} %get-tuple-element.714, bf16[8,32768]{1,0:T(8,128)(2,1)S(1)} %get-tuple-element.724, s32[]{:T(128)S(6)} %select_n.36, pred[]{:T(512)S(6)} %compare.12), kind=kOutput, calls=%fused_computation.9.clone.1 | convolution fusion | flops 62930944 | bytes 106505 | tf_op jit(solution)/shard_map/while/body/eval_jaxpr/dot_general | solution.py:38
  88.2 4.9 %fusion.114 = f32[8,1024]{1,0:T(8,128)S(1)} fusion(s32[]{:T(128)} %bitcast.37, s32[2048]{0:T(1024)S(1)} %add_multiply_fusion.8, f32[8,1024]{1,0:T(8,128)S(1)} %get-tuple-element.714, bf16[8,32768]{1,0:T(8,128)(2,1)S(1)} %get-tuple-element.724, s32[]{:T(128)S(6)} %select_n.36, pred[]{:T(512)S(6)} %compare.12), kind=kOutput, calls=%fused_computation.9.clone.1 | convolution fusion | flops 62930944 | bytes 106505 | tf_op jit(solution)/shard_map/while/body/eval_jaxpr/dot_general | solution.py:38
  93.1 4.9 %fusion.114 = f32[8,1024]{1,0:T(8,128)S(1)} fusion(s32[]{:T(128)} %bitcast.37, s32[2048]{0:T(1024)S(1)} %add_multiply_fusion.8, f32[8,1024]{1,0:T(8,128)S(1)} %get-tuple-element.714, bf16[8,32768]{1,0:T(8,128)(2,1)S(1)} %get-tuple-element.724, s32[]{:T(128)S(6)} %select_n.36, pred[]{:T(512)S(6)} %compare.12), kind=kOutput, calls=%fused_computation.9.clone.1 | convolution fusion | flops 62930944 | bytes 106505 | tf_op jit(solution)/shard_map/while/body/eval_jaxpr/dot_general | solution.py:38
  98.1 4.9 %fusion.114 = f32[8,1024]{1,0:T(8,128)S(1)} fusion(s32[]{:T(128)} %bitcast.37, s32[2048]{0:T(1024)S(1)} %add_multiply_fusion.8, f32[8,1024]{1,0:T(8,128)S(1)} %get-tuple-element.714, bf16[8,32768]{1,0:T(8,128)(2,1)S(1)} %get-tuple-element.724, s32[]{:T(128)S(6)} %select_n.36, pred[]{:T(512)S(6)} %compare.12), kind=kOutput, calls=%fused_computation.9.clone.1 | convolution fusion | flops 62930944 | bytes 106505 | tf_op jit(solution)/shard_map/while/body/eval_jaxpr/dot_general | solution.py:38
  103.0 4.9 %fusion.114 = f32[8,1024]{1,0:T(8,128)S(1)} fusion(s32[]{:T(128)} %bitcast.37, s32[2048]{0:T(1024)S(1)} %add_multiply_fusion.8, f32[8,1024]{1,0:T(8,128)S(1)} %get-tuple-element.714, bf16[8,32768]{1,0:T(8,128)(2,1)S(1)} %get-tuple-element.724, s32[]{:T(128)S(6)} %select_n.36, pred[]{:T(512)S(6)} %compare.12), kind=kOutput, calls=%fused_computation.9.clone.1 | convolution fusion | flops 62930944 | bytes 106505 | tf_op jit(solution)/shard_map/while/body/eval_jaxpr/dot_general | solution.py:38
  107.9 4.9 %fusion.114 = f32[8,1024]{1,0:T(8,128)S(1)} fusion(s32[]{:T(128)} %bitcast.37, s32[2048]{0:T(1024)S(1)} %add_multiply_fusion.8, f32[8,1024]{1,0:T(8,128)S(1)} %get-tuple-element.714, bf16[8,32768]{1,0:T(8,128)(2,1)S(1)} %get-tuple-element.724, s32[]{:T(128)S(6)} %select_n.36, pred[]{:T(512)S(6)} %compare.12), kind=kOutput, calls=%fused_computation.9.clone.1 | convolution fusion | flops 62930944 | bytes 106505 | tf_op jit(solution)/shard_map/while/body/eval_jaxpr/dot_general | solution.py:38
  112.8 76.3 %while.57 = (s32[]{:T(128)}, f32[8,1024]{1,0:T(8,128)S(1)}, bf16[8,32768]{1,0:T(8,128)(2,1)S(1)}, s32[]{:T(128)}, s32[1]{0:T(128)}, /*index=5*/s32[]{:T(128)}, s32[]{:T(128)}, s32[]{:T(128)}, s32[]{:T(128)}) while((s32[]{:T(128)}, f32[8,1024]{1,0:T(8,128)S(1)}, bf16[8,32768]{1,0:T(8,128)(2,1)S(1)}, s32[]{:T(128)}, s32[1]{0:T(128)}, ...), condition=%wide.region_3.0_spmd.clone, body=%wide.region_2.0_spmd.clone.sunk | while | flops 62936072 | bytes 123053 | solution.py:41
  112.8 4.8 %fusion.117 = f32[8,1024]{1,0:T(8,128)S(1)} fusion(s32[]{:T(128)} %bitcast.38, s32[1024]{0:T(1024)S(1)} %iota_add_fusion.6, s32[2048]{0:T(1024)S(1)} %add_multiply_fusion.9, f32[8,1024]{1,0:T(8,128)S(1)} %get-tuple-element.687, bf16[8,32768]{1,0:T(8,128)(2,1)S(1)} %get-tuple-element.697, s32[]{:T(128)S(6)} %select_n.37, pred[]{:T(512)S(6)} %compare.13), kind=kOutput, calls=%fused_computation.29.clone.1 | convolution fusion | flops 62930944 | bytes 110601 | tf_op jit(solution)/shard_map/while/body/eval_jaxpr/dot_general | solution.py:38
  117.6 4.8 %fusion.117 = f32[8,1024]{1,0:T(8,128)S(1)} fusion(s32[]{:T(128)} %bitcast.38, s32[1024]{0:T(1024)S(1)} %iota_add_fusion.6, s32[2048]{0:T(1024)S(1)} %add_multiply_fusion.9, f32[8,1024]{1,0:T(8,128)S(1)} %get-tuple-element.687, bf16[8,32768]{1,0:T(8,128)(2,1)S(1)} %get-tuple-element.697, s32[]{:T(128)S(6)} %select_n.37, pred[]{:T(512)S(6)} %compare.13), kind=kOutput, calls=%fused_computation.29.clone.1 | convolution fusion | flops 62930944 | bytes 110601 | tf_op jit(solution)/shard_map/while/body/eval_jaxpr/dot_general | solution.py:38
  122.4 4.8 %fusion.117 = f32[8,1024]{1,0:T(8,128)S(1)} fusion(s32[]{:T(128)} %bitcast.38, s32[1024]{0:T(1024)S(1)} %iota_add_fusion.6, s32[2048]{0:T(1024)S(1)} %add_multiply_fusion.9, f32[8,1024]{1,0:T(8,128)S(1)} %get-tuple-element.687, bf16[8,32768]{1,0:T(8,128)(2,1)S(1)} %get-tuple-element.697, s32[]{:T(128)S(6)} %select_n.37, pred[]{:T(512)S(6)} %compare.13), kind=kOutput, calls=%fused_computation.29.clone.1 | convolution fusion | flops 62930944 | bytes 110601 | tf_op jit(solution)/shard_map/while/body/eval_jaxpr/dot_general | solution.py:38
  127.1 4.8 %fusion.117 = f32[8,1024]{1,0:T(8,128)S(1)} fusion(s32[]{:T(128)} %bitcast.38, s32[1024]{0:T(1024)S(1)} %iota_add_fusion.6, s32[2048]{0:T(1024)S(1)} %add_multiply_fusion.9, f32[8,1024]{1,0:T(8,128)S(1)} %get-tuple-element.687, bf16[8,32768]{1,0:T(8,128)(2,1)S(1)} %get-tuple-element.697, s32[]{:T(128)S(6)} %select_n.37, pred[]{:T(512)S(6)} %compare.13), kind=kOutput, calls=%fused_computation.29.clone.1 | convolution fusion | flops 62930944 | bytes 110601 | tf_op jit(solution)/shard_map/while/body/eval_jaxpr/dot_general | solution.py:38
  131.9 4.8 %fusion.117 = f32[8,1024]{1,0:T(8,128)S(1)} fusion(s32[]{:T(128)} %bitcast.38, s32[1024]{0:T(1024)S(1)} %iota_add_fusion.6, s32[2048]{0:T(1024)S(1)} %add_multiply_fusion.9, f32[8,1024]{1,0:T(8,128)S(1)} %get-tuple-element.687, bf16[8,32768]{1,0:T(8,128)(2,1)S(1)} %get-tuple-element.697, s32[]{:T(128)S(6)} %select_n.37, pred[]{:T(512)S(6)} %compare.13), kind=kOutput, calls=%fused_computation.29.clone.1 | convolution fusion | flops 62930944 | bytes 110601 | tf_op jit(solution)/shard_map/while/body/eval_jaxpr/dot_general | solution.py:38
  136.7 4.8 %fusion.117 = f32[8,1024]{1,0:T(8,128)S(1)} fusion(s32[]{:T(128)} %bitcast.38, s32[1024]{0:T(1024)S(1)} %iota_add_fusion.6, s32[2048]{0:T(1024)S(1)} %add_multiply_fusion.9, f32[8,1024]{1,0:T(8,128)S(1)} %get-tuple-element.687, bf16[8,32768]{1,0:T(8,128)(2,1)S(1)} %get-tuple-element.697, s32[]{:T(128)S(6)} %select_n.37, pred[]{:T(512)S(6)} %compare.13), kind=kOutput, calls=%fused_computation.29.clone.1 | convolution fusion | flops 62930944 | bytes 110601 | tf_op jit(solution)/shard_map/while/body/eval_jaxpr/dot_general | solution.py:38
  141.4 4.8 %fusion.117 = f32[8,1024]{1,0:T(8,128)S(1)} fusion(s32[]{:T(128)} %bitcast.38, s32[1024]{0:T(1024)S(1)} %iota_add_fusion.6, s32[2048]{0:T(1024)S(1)} %add_multiply_fusion.9, f32[8,1024]{1,0:T(8,128)S(1)} %get-tuple-element.687, bf16[8,32768]{1,0:T(8,128)(2,1)S(1)} %get-tuple-element.697, s32[]{:T(128)S(6)} %select_n.37, pred[]{:T(512)S(6)} %compare.13), kind=kOutput, calls=%fused_computation.29.clone.1 | convolution fusion | flops 62930944 | bytes 110601 | tf_op jit(solution)/shard_map/while/body/eval_jaxpr/dot_general | solution.py:38
  146.2 4.8 %fusion.117 = f32[8,1024]{1,0:T(8,128)S(1)} fusion(s32[]{:T(128)} %bitcast.38, s32[1024]{0:T(1024)S(1)} %iota_add_fusion.6, s32[2048]{0:T(1024)S(1)} %add_multiply_fusion.9, f32[8,1024]{1,0:T(8,128)S(1)} %get-tuple-element.687, bf16[8,32768]{1,0:T(8,128)(2,1)S(1)} %get-tuple-element.697, s32[]{:T(128)S(6)} %select_n.37, pred[]{:T(512)S(6)} %compare.13), kind=kOutput, calls=%fused_computation.29.clone.1 | convolution fusion | flops 62930944 | bytes 110601 | tf_op jit(solution)/shard_map/while/body/eval_jaxpr/dot_general | solution.py:38
  151.0 4.8 %fusion.117 = f32[8,1024]{1,0:T(8,128)S(1)} fusion(s32[]{:T(128)} %bitcast.38, s32[1024]{0:T(1024)S(1)} %iota_add_fusion.6, s32[2048]{0:T(1024)S(1)} %add_multiply_fusion.9, f32[8,1024]{1,0:T(8,128)S(1)} %get-tuple-element.687, bf16[8,32768]{1,0:T(8,128)(2,1)S(1)} %get-tuple-element.697, s32[]{:T(128)S(6)} %select_n.37, pred[]{:T(512)S(6)} %compare.13), kind=kOutput, calls=%fused_computation.29.clone.1 | convolution fusion | flops 62930944 | bytes 110601 | tf_op jit(solution)/shard_map/while/body/eval_jaxpr/dot_general | solution.py:38
  155.7 4.8 %fusion.117 = f32[8,1024]{1,0:T(8,128)S(1)} fusion(s32[]{:T(128)} %bitcast.38, s32[1024]{0:T(1024)S(1)} %iota_add_fusion.6, s32[2048]{0:T(1024)S(1)} %add_multiply_fusion.9, f32[8,1024]{1,0:T(8,128)S(1)} %get-tuple-element.687, bf16[8,32768]{1,0:T(8,128)(2,1)S(1)} %get-tuple-element.697, s32[]{:T(128)S(6)} %select_n.37, pred[]{:T(512)S(6)} %compare.13), kind=kOutput, calls=%fused_computation.29.clone.1 | convolution fusion | flops 62930944 | bytes 110601 | tf_op jit(solution)/shard_map/while/body/eval_jaxpr/dot_general | solution.py:38
  160.5 4.8 %fusion.117 = f32[8,1024]{1,0:T(8,128)S(1)} fusion(s32[]{:T(128)} %bitcast.38, s32[1024]{0:T(1024)S(1)} %iota_add_fusion.6, s32[2048]{0:T(1024)S(1)} %add_multiply_fusion.9, f32[8,1024]{1,0:T(8,128)S(1)} %get-tuple-element.687, bf16[8,32768]{1,0:T(8,128)(2,1)S(1)} %get-tuple-element.697, s32[]{:T(128)S(6)} %select_n.37, pred[]{:T(512)S(6)} %compare.13), kind=kOutput, calls=%fused_computation.29.clone.1 | convolution fusion | flops 62930944 | bytes 110601 | tf_op jit(solution)/shard_map/while/body/eval_jaxpr/dot_general | solution.py:38
  165.3 4.8 %fusion.117 = f32[8,1024]{1,0:T(8,128)S(1)} fusion(s32[]{:T(128)} %bitcast.38, s32[1024]{0:T(1024)S(1)} %iota_add_fusion.6, s32[2048]{0:T(1024)S(1)} %add_multiply_fusion.9, f32[8,1024]{1,0:T(8,128)S(1)} %get-tuple-element.687, bf16[8,32768]{1,0:T(8,128)(2,1)S(1)} %get-tuple-element.697, s32[]{:T(128)S(6)} %select_n.37, pred[]{:T(512)S(6)} %compare.13), kind=kOutput, calls=%fused_computation.29.clone.1 | convolution fusion | flops 62930944 | bytes 110601 | tf_op jit(solution)/shard_map/while/body/eval_jaxpr/dot_general | solution.py:38
  170.0 4.8 %fusion.117 = f32[8,1024]{1,0:T(8,128)S(1)} fusion(s32[]{:T(128)} %bitcast.38, s32[1024]{0:T(1024)S(1)} %iota_add_fusion.6, s32[2048]{0:T(1024)S(1)} %add_multiply_fusion.9, f32[8,1024]{1,0:T(8,128)S(1)} %get-tuple-element.687, bf16[8,32768]{1,0:T(8,128)(2,1)S(1)} %get-tuple-element.697, s32[]{:T(128)S(6)} %select_n.37, pred[]{:T(512)S(6)} %compare.13), kind=kOutput, calls=%fused_computation.29.clone.1 | convolution fusion | flops 62930944 | bytes 110601 | tf_op jit(solution)/shard_map/while/body/eval_jaxpr/dot_general | solution.py:38
  174.8 4.8 %fusion.117 = f32[8,1024]{1,0:T(8,128)S(1)} fusion(s32[]{:T(128)} %bitcast.38, s32[1024]{0:T(1024)S(1)} %iota_add_fusion.6, s32[2048]{0:T(1024)S(1)} %add_multiply_fusion.9, f32[8,1024]{1,0:T(8,128)S(1)} %get-tuple-element.687, bf16[8,32768]{1,0:T(8,128)(2,1)S(1)} %get-tuple-element.697, s32[]{:T(128)S(6)} %select_n.37, pred[]{:T(512)S(6)} %compare.13), kind=kOutput, calls=%fused_computation.29.clone.1 | convolution fusion | flops 62930944 | bytes 110601 | tf_op jit(solution)/shard_map/while/body/eval_jaxpr/dot_general | solution.py:38
  189.1 76.4 %while.58 = (s32[]{:T(128)}, f32[8,1024]{1,0:T(8,128)S(1)}, bf16[8,32768]{1,0:T(8,128)(2,1)S(1)}, s32[]{:T(128)}, s32[1]{0:T(128)}, /*index=5*/s32[]{:T(128)}, s32[]{:T(128)}, s32[]{:T(128)}, s32[]{:T(128)}) while((s32[]{:T(128)}, f32[8,1024]{1,0:T(8,128)S(1)}, bf16[8,32768]{1,0:T(8,128)(2,1)S(1)}, s32[]{:T(128)}, s32[1]{0:T(128)}, ...), condition=%wide.region_5.0_spmd.clone, body=%wide.region_4.0_spmd.clone.sunk | while | flops 62936072 | bytes 123053 | solution.py:41
  189.2 4.8 %fusion.120 = f32[8,1024]{1,0:T(8,128)S(1)} fusion(s32[]{:T(128)} %bitcast.39, s32[1024]{0:T(1024)S(1)} %iota_add_fusion.7, s32[2048]{0:T(1024)S(1)} %add_multiply_fusion.10, f32[8,1024]{1,0:T(8,128)S(1)} %get-tuple-element.660, bf16[8,32768]{1,0:T(8,128)(2,1)S(1)} %get-tuple-element.670, s32[]{:T(128)S(6)} %select_n.38, pred[]{:T(512)S(6)} %compare.14), kind=kOutput, calls=%fused_computation.50.clone.1 | convolution fusion | flops 62930944 | bytes 110601 | tf_op jit(solution)/shard_map/while/body/eval_jaxpr/dot_general | solution.py:38
  194.0 4.8 %fusion.120 = f32[8,1024]{1,0:T(8,128)S(1)} fusion(s32[]{:T(128)} %bitcast.39, s32[1024]{0:T(1024)S(1)} %iota_add_fusion.7, s32[2048]{0:T(1024)S(1)} %add_multiply_fusion.10, f32[8,1024]{1,0:T(8,128)S(1)} %get-tuple-element.660, bf16[8,32768]{1,0:T(8,128)(2,1)S(1)} %get-tuple-element.670, s32[]{:T(128)S(6)} %select_n.38, pred[]{:T(512)S(6)} %compare.14), kind=kOutput, calls=%fused_computation.50.clone.1 | convolution fusion | flops 62930944 | bytes 110601 | tf_op jit(solution)/shard_map/while/body/eval_jaxpr/dot_general | solution.py:38
  217.8 4.8 %fusion.120 = f32[8,1024]{1,0:T(8,128)S(1)} fusion(s32[]{:T(128)} %bitcast.39, s32[1024]{0:T(1024)S(1)} %iota_add_fusion.7, s32[2048]{0:T(1024)S(1)} %add_multiply_fusion.10, f32[8,1024]{1,0:T(8,128)S(1)} %get-tuple-element.660, bf16[8,32768]{1,0:T(8,128)(2,1)S(1)} %get-tuple-element.670, s32[]{:T(128)S(6)} %select_n.38, pred[]{:T(512)S(6)} %compare.14), kind=kOutput, calls=%fused_computation.50.clone.1 | convolution fusion | flops 62930944 | bytes 110601 | tf_op jit(solution)/shard_map/while/body/eval_jaxpr/dot_general | solution.py:38
  222.6 4.8 %fusion.120 = f32[8,1024]{1,0:T(8,128)S(1)} fusion(s32[]{:T(128)} %bitcast.39, s32[1024]{0:T(1024)S(1)} %iota_add_fusion.7, s32[2048]{0:T(1024)S(1)} %add_multiply_fusion.10, f32[8,1024]{1,0:T(8,128)S(1)} %get-tuple-element.660, bf16[8,32768]{1,0:T(8,128)(2,1)S(1)} %get-tuple-element.670, s32[]{:T(128)S(6)} %select_n.38, pred[]{:T(512)S(6)} %compare.14), kind=kOutput, calls=%fused_computation.50.clone.1 | convolution fusion | flops 62930944 | bytes 110601 | tf_op jit(solution)/shard_map/while/body/eval_jaxpr/dot_general | solution.py:38
  246.4 4.8 %fusion.120 = f32[8,1024]{1,0:T(8,128)S(1)} fusion(s32[]{:T(128)} %bitcast.39, s32[1024]{0:T(1024)S(1)} %iota_add_fusion.7, s32[2048]{0:T(1024)S(1)} %add_multiply_fusion.10, f32[8,1024]{1,0:T(8,128)S(1)} %get-tuple-element.660, bf16[8,32768]{1,0:T(8,128)(2,1)S(1)} %get-tuple-element.670, s32[]{:T(128)S(6)} %select_n.38, pred[]{:T(512)S(6)} %compare.14), kind=kOutput, calls=%fused_computation.50.clone.1 | convolution fusion | flops 62930944 | bytes 110601 | tf_op jit(solution)/shard_map/while/body/eval_jaxpr/dot_general | solution.py:38
  251.2 4.8 %fusion.120 = f32[8,1024]{1,0:T(8,128)S(1)} fusion(s32[]{:T(128)} %bitcast.39, s32[1024]{0:T(1024)S(1)} %iota_add_fusion.7, s32[2048]{0:T(1024)S(1)} %add_multiply_fusion.10, f32[8,1024]{1,0:T(8,128)S(1)} %get-tuple-element.660, bf16[8,32768]{1,0:T(8,128)(2,1)S(1)} %get-tuple-element.670, s32[]{:T(128)S(6)} %select_n.38, pred[]{:T(512)S(6)} %compare.14), kind=kOutput, calls=%fused_computation.50.clone.1 | convolution fusion | flops 62930944 | bytes 110601 | tf_op jit(solution)/shard_map/while/body/eval_jaxpr/dot_general | solution.py:38
  265.5 76.3 %while.59 = (s32[]{:T(128)}, f32[8,1024]{1,0:T(8,128)S(1)}, bf16[8,32768]{1,0:T(8,128)(2,1)S(1)}, s32[]{:T(128)}, s32[1]{0:T(128)}, /*index=5*/s32[]{:T(128)}, s32[]{:T(128)}, s32[]{:T(128)}, s32[]{:T(128)}) while((s32[]{:T(128)}, f32[8,1024]{1,0:T(8,128)S(1)}, bf16[8,32768]{1,0:T(8,128)(2,1)S(1)}, s32[]{:T(128)}, s32[1]{0:T(128)}, ...), condition=%wide.region_7.0_spmd.clone, body=%wide.region_6.0_spmd.clone.sunk | while | flops 62936072 | bytes 123053 | solution.py:41
  284.6 4.8 %fusion.123 = f32[8,1024]{1,0:T(8,128)S(1)} fusion(s32[]{:T(128)} %bitcast.40, s32[1024]{0:T(1024)S(1)} %iota_add_fusion.8, s32[2048]{0:T(1024)S(1)} %add_multiply_fusion.11, f32[8,1024]{1,0:T(8,128)S(1)} %get-tuple-element.633, bf16[8,32768]{1,0:T(8,128)(2,1)S(1)} %get-tuple-element.643, s32[]{:T(128)S(6)} %select_n.39, pred[]{:T(512)S(6)} %compare.15), kind=kOutput, calls=%fused_computation.71.clone.1 | convolution fusion | flops 62930944 | bytes 110601 | tf_op jit(solution)/shard_map/while/body/eval_jaxpr/dot_general | solution.py:38
  289.3 4.8 %fusion.123 = f32[8,1024]{1,0:T(8,128)S(1)} fusion(s32[]{:T(128)} %bitcast.40, s32[1024]{0:T(1024)S(1)} %iota_add_fusion.8, s32[2048]{0:T(1024)S(1)} %add_multiply_fusion.11, f32[8,1024]{1,0:T(8,128)S(1)} %get-tuple-element.633, bf16[8,32768]{1,0:T(8,128)(2,1)S(1)} %get-tuple-element.643, s32[]{:T(128)S(6)} %select_n.39, pred[]{:T(512)S(6)} %compare.15), kind=kOutput, calls=%fused_computation.71.clone.1 | convolution fusion | flops 62930944 | bytes 110601 | tf_op jit(solution)/shard_map/while/body/eval_jaxpr/dot_general | solution.py:38
  313.2 4.8 %fusion.123 = f32[8,1024]{1,0:T(8,128)S(1)} fusion(s32[]{:T(128)} %bitcast.40, s32[1024]{0:T(1024)S(1)} %iota_add_fusion.8, s32[2048]{0:T(1024)S(1)} %add_multiply_fusion.11, f32[8,1024]{1,0:T(8,128)S(1)} %get-tuple-element.633, bf16[8,32768]{1,0:T(8,128)(2,1)S(1)} %get-tuple-element.643, s32[]{:T(128)S(6)} %select_n.39, pred[]{:T(512)S(6)} %compare.15), kind=kOutput, calls=%fused_computation.71.clone.1 | convolution fusion | flops 62930944 | bytes 110601 | tf_op jit(solution)/shard_map/while/body/eval_jaxpr/dot_general | solution.py:38
  317.9 4.8 %fusion.123 = f32[8,1024]{1,0:T(8,128)S(1)} fusion(s32[]{:T(128)} %bitcast.40, s32[1024]{0:T(1024)S(1)} %iota_add_fusion.8, s32[2048]{0:T(1024)S(1)} %add_multiply_fusion.11, f32[8,1024]{1,0:T(8,128)S(1)} %get-tuple-element.633, bf16[8,32768]{1,0:T(8,128)(2,1)S(1)} %get-tuple-element.643, s32[]{:T(128)S(6)} %select_n.39, pred[]{:T(512)S(6)} %compare.15), kind=kOutput, calls=%fused_computation.71.clone.1 | convolution fusion | flops 62930944 | bytes 110601 | tf_op jit(solution)/shard_map/while/body/eval_jaxpr/dot_general | solution.py:38
  337.0 4.8 %fusion.123 = f32[8,1024]{1,0:T(8,128)S(1)} fusion(s32[]{:T(128)} %bitcast.40, s32[1024]{0:T(1024)S(1)} %iota_add_fusion.8, s32[2048]{0:T(1024)S(1)} %add_multiply_fusion.11, f32[8,1024]{1,0:T(8,128)S(1)} %get-tuple-element.633, bf16[8,32768]{1,0:T(8,128)(2,1)S(1)} %get-tuple-element.643, s32[]{:T(128)S(6)} %select_n.39, pred[]{:T(512)S(6)} %compare.15), kind=kOutput, calls=%fused_computation.71.clone.1 | convolution fusion | flops 62930944 | bytes 110601 | tf_op jit(solution)/shard_map/while/body/eval_jaxpr/dot_general | solution.py:38
  343.0 52.4 %all-reduce.3.cloned.1.call-done = f32[8,4096]{1,0:T(8,128)} async-done(((f32[8,4096]{1,0:T(8,128)}), f32[8,4096]{1,0:T(8,128)}) %all-reduce.3.cloned.1.call-update) | async-done | bytes 131088
  (163 shorter events, 119.4 us)
Async XLA Ops:
  6.5 1.1 copy-start
  6.5 2.8 copy-start.1
  6.5 2.8 copy-start.2
  12.4 5.6 %copy-start.3 = (f32[32768]{0:T(1024)S(1)}, f32[32768]{0:T(1024)}, u32[]{:S(2)}) copy-start(f32[32768]{0:T(1024)} %param.21) | copy-start | bytes 393220
  12.4 5.6 %copy-start.4 = (f32[32768]{0:T(1024)S(1)}, f32[32768]{0:T(1024)}, u32[]{:S(2)}) copy-start(f32[32768]{0:T(1024)} %param.20) | copy-start | bytes 393220
  12.4 20.7 %all-to-all-start = ((f32[1,8,32768]{2,0,1:T(1,128)}), f32[1,8,32768]{2,0,1:T(1,128)S(1)}, u32[]{:S(2)}, u32[]{:S(2)}) async-start(f32[1,8,32768]{2,0,1:T(1,128)} %all_to_all.15), calls=%async_computation | async-start | bytes 2097152 | tf_op jit(solution)/shard_map/all_to_all | solution.py:72
  17.7 377.7 %all-reduce.3.cloned.1.call-start = ((), (), s32[]{:S(2)}) async-start(), calls=%async_computation.1 | async-start | bytes 262144
  265.5 76.9 %copy-start.5 = (u32[32]{0:T(128)S(1)}, u32[32]{0:T(128)}, u32[]{:S(2)}) copy-start(u32[32]{0:T(128)} %constant.324) | copy-start | bytes 388
Sparse Core Ops, SparseCore 0:
  342.5 52.8 all-reduce.2
where the time goes:
time: 405 us; the launch traced here: 404 us
  matrix products  309 us (76%)
  waiting for transfers between devices  67.5 us (17%)
  between operations  14.3 us (4%)
  starting transfers between devices  5.55 us (1%)
  other arithmetic  4.32 us (1%)
    dot_general x64, matrix products, add_block(): return total + jnp.dot(rows, signs, preferred_element_type=jnp.float32)  307 us
    unnamed x2, waiting for transfers between devices  52.4 us
    all_to_all x1, waiting for transfers between devices, body(): lax.all_to_all(grads, 'narrow', split_axis=1, concat_axis=0, tiled=True)  15.1 us
  transfers between devices with their start and end apart: 2, of which 2 were waited for; matrix products, arithmetic and copies ran while one was open for 0% of the time, Pallas kernels for 0%

commit v1 on v0

v1 whole, which is shorter than its diff:
```python
import functools
import math

import jax
import jax.numpy as jnp
import numpy as np
from jax import lax
from jax.experimental import pallas as pl
from jax.experimental.pallas import tpu as pltpu
from jax.sharding import PartitionSpec as P

FEAT = 4096
MUL_A = 747796405
MUL_B = 277803737
AXES = ("wide", "narrow")
COLUMN_BITS = 11
LOW = (1 << COLUMN_BITS) - 1
TILE = 256
I16 = jnp.int16
I32 = jnp.int32


def short(value):
    value &= 0xFFFF
    return np.int16(value - 65536 if value >= 32768 else value)


def grads_kernel(length_ref, acts_ref, cot_ref, down_ref, up_ref, grads_ref):
    rank = down_ref.shape[0]
    acts = acts_ref[...]
    slots = lax.broadcasted_iota(I32, cot_ref.shape, 0)
    masked = jnp.where(slots < length_ref[0], cot_ref[...].astype(jnp.float32), 0.0)
    masked = masked.astype(jnp.bfloat16)
    last = (((1,), (1,)), ((), ()))
    first = (((0,), (0,)), ((), ()))
    hidden = lax.dot_general(acts, down_ref[...], last, preferred_element_type=jnp.float32)
    inner = jnp.dot(masked, up_ref[...], preferred_element_type=jnp.float32)
    grads_ref[:rank, :] = lax.dot_general(
        inner.astype(jnp.bfloat16), acts, first, preferred_element_type=jnp.float32
    )
    grads_ref[rank:, :] = lax.dot_general(
        hidden.astype(jnp.bfloat16), masked, first, preferred_element_type=jnp.float32
    )


def sequence_grads(acts, cotangent, down_matrix, up_matrix, lengths):
    rank, inputs = down_matrix.shape
    vmem = pl.BlockSpec(memory_space=pltpu.VMEM)
    return pl.pallas_call(
        grads_kernel,
        out_shape=jax.ShapeDtypeStruct((2 * rank, inputs), jnp.float32),
        in_specs=[pl.BlockSpec(memory_space=pltpu.SMEM)] + [vmem] * 4,
        out_specs=vmem,
        name="grads",
    )(lengths, acts[0], cotangent[0], down_matrix, up_matrix)


def lane_terms(info_ref, tile):
    salt = info_ref[0]
    feature = lax.broadcasted_iota(I32, (8, TILE), 1) + tile * TILE
    product = (feature ^ (salt & (FEAT - 1))) * MUL_A + 1
    low = product & (FEAT - 1)
    high = lax.shift_right_logical(product, 12)

    def packed(x):
        return jnp.concatenate([x, x], 0).astype(I16)

    return (
        packed(high & LOW),
        packed(((high >> COLUMN_BITS) & 511) + 256),
        packed(low >> 8),
        packed((low & 255) << 3),
    )


def column_terms(info_ref, lanes, block):
    lane_low, lane_high, lane_top, lane_byte = lanes
    salt_row = info_ref[0] >> 12
    column = lax.broadcasted_iota(I32, (16, 128), 0) + (info_ref[2] + block * 16)
    product = ((column ^ (salt_row & LOW)) * MUL_A) & 0xFFFFF
    row_low = (product & LOW).astype(I16)
    row_high = (product >> COLUMN_BITS).astype(I16)
    wide = (1, TILE // 128)
    row_low, row_high = jnp.tile(row_low, wide), jnp.tile(row_high, wide)
    total = row_low + lane_low
    height = row_high + lane_high + lax.shift_right_logical(total, I16(COLUMN_BITS))
    mixed = total * I16(16) + lane_top
    byte8 = (total ^ lane_byte) & I16(0x7F8)
    byte = lax.shift_right_logical(byte8, I16(3))
    tail = byte * I16(MUL_B & 255)
    carry = byte8 * short(MUL_B >> 8) + lax.shift_right_logical(tail, I16(5))
    carry = carry + ((tail * I16(256)) & I16(-32768))
    return height, mixed, carry


def row_heights(info_ref, rows):
    return [
        (((info_ref[1] + k) ^ (info_ref[0] >> (12 + COLUMN_BITS))) * MUL_A) & 511
        for k in range(rows)
    ]


def regroup(updates_ref, grouped_ref, rows, columns):
    lane = lax.broadcasted_iota(I32, (updates_ref.shape[0], 128), 1)
    for half in range(rows // 8):
        for part in range(columns // 128):
            pieces = [
                updates_ref[:, pl.ds((half * 8 + k) * columns + part * 128, 128)]
                for k in range(8)
            ]
            for step in (4, 2, 1):
                upper = ((lane // 16) & step) != 0
                for k in range(8):
                    if k & step:
                        continue
                    a, b = pieces[k], pieces[k + step]
                    pieces[k] = jnp.where(upper, pltpu.roll(b, 16 * step, 1), a)
                    pieces[k + step] = jnp.where(upper, b, pltpu.roll(a, 128 - 16 * step, 1))
            for c in range(8):
                grouped_ref[part * 8 + c, :, half * 128 : half * 128 + 128] = pieces[c].astype(
                    jnp.bfloat16
                )


def project_kernel(rows, columns, info_ref, updates_ref, out_ref, grouped_ref):
    tile = pl.program_id(0)

    @pl.when(tile == 0)
    def _():
        if columns:
            regroup(updates_ref, grouped_ref, rows, columns)
        else:
            grouped_ref[...] = updates_ref[...].astype(jnp.bfloat16)

    lanes = lane_terms(info_ref, tile)
    heights = row_heights(info_ref, rows)
    heights = [jnp.full((16, TILE), h, I32).astype(I16) for h in heights]

    def add_block(block, total):
        height, mixed, carry = column_terms(info_ref, lanes, block)
        signs = []
        for k in range(rows):
            value = (((height + heights[k]) & I16(511)) - I16(256)) ^ mixed
            value = value * short(8 * MUL_B) + carry
            signs.append(jnp.where(value < 0, jnp.bfloat16(-1), jnp.bfloat16(1)))
        signs = jnp.concatenate(signs, 0)
        return total + jnp.dot(grouped_ref[block], signs, preferred_element_type=jnp.float32)

    out_ref[...] = lax.fori_loop(
        0, grouped_ref.shape[0], add_block, jnp.zeros(out_ref.shape, jnp.float32)
    )


def project(info, updates):
    m, rows, columns = updates.shape
    blocks = columns // 16
    if rows % 8 == 0 and columns % 128 == 0:
        flat = updates.reshape(m, rows * columns)
        inside = columns
    else:
        flat = updates.reshape(m, rows, blocks, 16).transpose(2, 0, 1, 3)
        flat = flat.reshape(blocks, m, rows * 16)
        inside = 0
    whole = pl.BlockSpec(flat.shape, lambda t, i: (0,) * flat.ndim)
    return pl.pallas_call(
        functools.partial(project_kernel, rows, inside),
        out_shape=jax.ShapeDtypeStruct((m, FEAT), jnp.float32),
        grid_spec=pltpu.PrefetchScalarGridSpec(
            num_scalar_prefetch=1,
            grid=(FEAT // TILE,),
            in_specs=[whole],
            out_specs=pl.BlockSpec((m, TILE), lambda t, i: (0, t)),
            scratch_shapes=[pltpu.VMEM((blocks, m, rows * 16), jnp.bfloat16)],
        ),
        name="project",
    )(info, flat)


def body(
    groups,
    holders,
    acts,
    cotangent,
    down_matrix,
    up_matrix,
    adam_first_moment,
    adam_second_moment,
    lengths,
    sign_hash_salt,
):
    rank, inputs = down_matrix.shape
    rank_rows = 2 * rank
    rows, columns = rank_rows // holders, inputs // groups
    devices = groups * holders
    params = rank_rows * inputs
    bound = acts.shape[1] * inputs * 6 * 0.125 * 0.5
    scale = 2.0 ** -max(0, math.ceil(math.log2(bound / 60000)))
    group, holder = lax.axis_index("wide"), lax.axis_index("narrow")

    grads = sequence_grads(acts, cotangent, down_matrix, up_matrix, lengths)
    sent = (grads * scale).astype(jnp.float16).reshape(holders, rows, groups, columns)
    sent = sent.transpose(2, 0, 1, 3).reshape(devices, rows, columns)
    grads = lax.all_to_all(sent, AXES, 0, 0, tiled=True).astype(jnp.float32) * (1 / scale)

    def share(moment):
        return lax.dynamic_slice_in_dim(moment.reshape(rows, inputs), group * columns, columns, 1)

    first, second = share(adam_first_moment), share(adam_second_moment)
    moment_one = 0.9 * first[None] + 0.1 * grads
    moment_two = 0.999 * second[None] + 0.001 * grads * grads
    updates = (moment_one / (jnp.sqrt(moment_two) + 1e-08)).astype(jnp.bfloat16)

    info = jnp.stack([sign_hash_salt[0], holder * rows, group * columns])
    partial = project(info, updates) * params**-0.5
    parts = lax.all_to_all(partial.astype(jnp.float16), AXES, 0, 0, tiled=True)
    return jnp.sum(parts.astype(jnp.float32), axis=0, keepdims=True)


def solution(mesh):
    groups, holders = mesh.shape["wide"], mesh.shape["narrow"]
    placed = (
        P(AXES, None, None),
        P(AXES, None, None),
        P(),
        P(),
        P("narrow"),
        P("narrow"),
        P(AXES),
        P(),
    )
    return jax.shard_map(
        functools.partial(body, groups, holders),
        mesh=mesh,
        in_specs=placed,
        out_specs=P(AXES, None),
        check_vma=False,
    )
```

time: 405 us -> 143 us (0.35)
  matrix products: 309 us -> 0 us
  Pallas kernels: 0 us -> 95.3 us
  waiting for transfers between devices: 67.5 us -> 13.3 us
  blocking collectives: 0 us -> 13.4 us
  between operations: 14.3 us -> 1.39 us
    dot_general x66 -> x0, matrix products: 309 us -> none  [the longest x64 307 us: add_block(): return total + jnp.dot(rows, signs, preferred_element_type=jnp.float32)]
    pallas_call x0 -> x2, Pallas kernels: none -> 95.3 us  [the longest x1 92.1 us: project(): pl.pallas_call(functools.partial(project_kernel, rows, inside), out_shape...]
    unnamed x2 -> x0, waiting for transfers between devices: 52.4 us -> none
    all_to_all x0 -> x1, blocking collectives: none -> 13.4 us  [body(): parts = lax.all_to_all(partial.astype(jnp.float16), AXES, 0, 0, tiled=True)]
  transfers between devices with their start and end apart: 2 -> 1, of which waited for: 2 -> 1; matrix products, arithmetic and copies ran while one was open for 0% -> 1% of each run, Pallas kernels for 0% -> 0%
where the time goes in v1:
time: 143 us
  Pallas kernels  95.3 us (67%)
  blocking collectives  13.4 us (9%)
  waiting for transfers between devices  13.3 us (9%)
  starting transfers between devices  7.32 us (5%)
  local copies, waits for them, and re-layouts  6.4 us (4%)
  other arithmetic  5.63 us (4%)
    pallas_call x1, Pallas kernels, project(): pl.pallas_call(functools.partial(project_kernel, rows, inside), out_shape...  92.1 us
    all_to_all x1, blocking collectives, body(): parts = lax.all_to_all(partial.astype(jnp.float16), AXES, 0, 0, tiled=True)  13.4 us
    all_to_all x1, waiting for transfers between devices, body(): lax.all_to_all(sent, AXES, 0, 0, tiled=True).astype(jnp.float32)  13.3 us
    all_to_all x1, starting transfers between devices, body(): lax.all_to_all(sent, AXES, 0, 0, tiled=True).astype(jnp.float32)  7.32 us
    unnamed x8, local copies, waits for them, and re-layouts  4.43 us
    pallas_call x1, Pallas kernels, sequence_grads(): pl.pallas_call(grads_kernel, out_shape=jax.ShapeDtypeStruct((2 * rank, in...  3.17 us
  transfers between devices with their start and end apart: 1, of which 1 were waited for; matrix products, arithmetic and copies ran while one was open for 1% of the time, Pallas kernels for 0%

profile of v1, /device:TPU:0, one launch (start us, length us, event | category | flops | bytes accessed | tf_op | source)
XLA Modules:
  0.0 142.7 jit_solution(14566869533621515929)
XLA Ops:
  0.7 2.0 %copy.11.up_ref = bf16[2048,64]{1,0:T(8,128)(2,1)} copy(bf16[2048,64]{0,1:T(8,128)(2,1)} %param.11) | data formatting | bytes 524288 | tf_op args[3]
  2.6 3.2 %grads.1 = f32[128,2048]{1,0:T(8,128)} custom-call(s32[1]{0:T(128)S(6)} %copy.16.length_ref, bf16[128,2048]{1,0:T(8,128)(2,1)} %bitcast.14, bf16[128,2048]{1,0:T(8,128)(2,1)} %bitcast.15, bf16[64,2048]{1,0:T(8,128)(2,1)} %down_ref.1, bf16[2048,64]{1,0:T(8,128)(2,1)} %copy.11.up_ref), custom_call_target="tpu_custom_call" | custom-call | tf_op jit(solution)/shard_map/grads/pallas_call | solution.py:49
  5.8 1.3 multiply_convert_fusion
  7.1 0.5 reshape.23
  7.6 0.9 copy.12
  8.5 0.0 copy-start
  8.5 7.3 %all-to-all-start = ((f16[32,16,512]{2,1,0:T(8,128)(2,1)}), f16[32,16,512]{2,1,0:T(8,128)(2,1)S(1)}, u32[]{:S(2)}, u32[]{:S(2)}) async-start(f16[32,16,512]{2,1,0:T(8,128)(2,1)} %bitcast.5), calls=%async_computation | async-start | bytes 1048576 | tf_op jit(solution)/shard_map/all_to_all | solution.py:203
  16.5 0.0 copy-done
  16.5 0.0 copy-start.1
  16.6 0.9 copy-done.1
  17.5 0.7 pad_add_fusion.info_ref
  18.1 13.3 %all-to-all-done = f16[32,16,512]{2,1,0:T(8,128)(2,1)S(1)} async-done(((f16[32,16,512]{2,1,0:T(8,128)(2,1)}), f16[32,16,512]{2,1,0:T(8,128)(2,1)S(1)}, u32[]{:S(2)}, u32[]{:S(2)}) %all-to-all-start) | async-done | bytes 524320 | tf_op jit(solution)/shard_map/all_to_all | solution.py:203
  31.5 0.6 fusion.2
  32.1 1.1 copy.14
  33.2 92.1 %project.1 = f32[32,4096]{1,0:T(8,128)} custom-call(s32[3]{0:T(128)} %pad_add_fusion.info_ref, bf16[32,8192]{1,0:T(8,128)(2,1)} %bitcast.12), custom_call_target="tpu_custom_call" | custom-call | tf_op jit(solution)/shard_map/project/pallas_call | solution.py:165
  125.3 1.1 fusion.7
  126.4 0.5 broadcast.6
  126.9 0.8 reduce.1
  127.7 0.2 reshape.27
  127.9 13.4 %all_to_all.14 = f16[32,2,2048]{2,1,0:T(2,128)(2,1)S(1)} all-to-all(f16[32,2,2048]{2,1,0:T(2,128)(2,1)S(1)} %reshape.27), channel_id=1, replica_groups=mesh['wide'=4,'narrow'=8] {'wide','narrow'}, dimensions={0} | all-to-all | bytes 524288 | tf_op jit(solution)/shard_map/all_to_all | solution.py:215
  141.2 0.3 reshape.28
  141.5 1.2 convert_reduce_fusion
  (3 shorter events, 0.1 us)
Async XLA Ops:
  8.5 8.0 %copy-start = (f32[32768]{0:T(1024)S(1)}, f32[32768]{0:T(1024)}, u32[]{:S(2)}) copy-start(f32[32768]{0:T(1024)} %param.13) | copy-start | bytes 393220
  8.5 22.9 %all-to-all-start = ((f16[32,16,512]{2,1,0:T(8,128)(2,1)}), f16[32,16,512]{2,1,0:T(8,128)(2,1)S(1)}, u32[]{:S(2)}, u32[]{:S(2)}) async-start(f16[32,16,512]{2,1,0:T(8,128)(2,1)} %bitcast.5), calls=%async_computation | async-start | bytes 1048576 | tf_op jit(solution)/shard_map/all_to_all | solution.py:203
  16.5 0.9 copy-start.1

commit v2 on v1

--- a/solution.py
+++ b/solution.py
@@ -15,7 +15,8 @@
 AXES = ("wide", "narrow")
 COLUMN_BITS = 11
 LOW = (1 << COLUMN_BITS) - 1
-TILE = 256
+TILE = 512
+GROUP = 32
 I16 = jnp.int16
 I32 = jnp.int32
 
@@ -25,8 +26,8 @@
     return np.int16(value - 65536 if value >= 32768 else value)
 
 
-def grads_kernel(length_ref, acts_ref, cot_ref, down_ref, up_ref, grads_ref):
-    rank = down_ref.shape[0]
+def grads_kernel(holders, length_ref, acts_ref, cot_ref, down_ref, up_ref, grads_ref):
+    groups, (rows, columns) = grads_ref.shape[0] // holders, grads_ref.shape[1:]
     acts = acts_ref[...]
     slots = lax.broadcasted_iota(I32, cot_ref.shape, 0)
     masked = jnp.where(slots < length_ref[0], cot_ref[...].astype(jnp.float32), 0.0)
@@ -34,25 +35,29 @@
     last = (((1,), (1,)), ((), ()))
     first = (((0,), (0,)), ((), ()))
     hidden = lax.dot_general(acts, down_ref[...], last, preferred_element_type=jnp.float32)
-    inner = jnp.dot(masked, up_ref[...], preferred_element_type=jnp.float32)
-    grads_ref[:rank, :] = lax.dot_general(
-        inner.astype(jnp.bfloat16), acts, first, preferred_element_type=jnp.float32
-    )
-    grads_ref[rank:, :] = lax.dot_general(
-        hidden.astype(jnp.bfloat16), masked, first, preferred_element_type=jnp.float32
-    )
-
-
-def sequence_grads(acts, cotangent, down_matrix, up_matrix, lengths):
+    inner = lax.dot_general(masked, up_ref[...], last, preferred_element_type=jnp.float32)
+    for half, (left, right) in enumerate(((inner, acts), (hidden, masked))):
+        grads = lax.dot_general(
+            left.astype(jnp.bfloat16), right, first, preferred_element_type=jnp.float32
+        )
+        for holder in range(holders // 2):
+            for group in range(groups):
+                grads_ref[group * holders + half * (holders // 2) + holder] = grads[
+                    holder * rows : (holder + 1) * rows, group * columns : (group + 1) * columns
+                ]
+
+
+def sequence_grads(groups, holders, acts, cotangent, down_matrix, up_matrix, lengths):
     rank, inputs = down_matrix.shape
     vmem = pl.BlockSpec(memory_space=pltpu.VMEM)
+    slabs = (groups * holders, 2 * rank // holders, inputs // groups)
     return pl.pallas_call(
-        grads_kernel,
-        out_shape=jax.ShapeDtypeStruct((2 * rank, inputs), jnp.float32),
+        functools.partial(grads_kernel, holders),
+        out_shape=jax.ShapeDtypeStruct(slabs, jnp.float32),
         in_specs=[pl.BlockSpec(memory_space=pltpu.SMEM)] + [vmem] * 4,
         out_specs=vmem,
         name="grads",
-    )(lengths, acts[0], cotangent[0], down_matrix, up_matrix)
+    )(lengths, acts[0], cotangent[0], down_matrix, up_matrix.T)
 
 
 def lane_terms(info_ref, tile):
@@ -100,12 +105,14 @@
     ]
 
 
-def regroup(updates_ref, grouped_ref, rows, columns):
-    lane = lax.broadcasted_iota(I32, (updates_ref.shape[0], 128), 1)
-    for half in range(rows // 8):
-        for part in range(columns // 128):
+def regroup(updates_ref, grouped_ref, staged_ref, rows, columns):
+    devices = grouped_ref.shape[1]
+    lane = lax.broadcasted_iota(I32, (devices, 128), 1)
+    for part in range(columns // 128):
+        staged_ref[...] = updates_ref[:, part * 128 : part * 128 + 128]
+        for half in range(rows // 8):
             pieces = [
-                updates_ref[:, pl.ds((half * 8 + k) * columns + part * 128, 128)]
+                staged_ref[pl.ds(half * 8 + k, devices, stride=rows), :]
                 for k in range(8)
             ]
             for step in (4, 2, 1):
@@ -122,13 +129,15 @@
                 )
 
 
-def project_kernel(rows, columns, info_ref, updates_ref, out_ref, grouped_ref):
+def project_kernel(
+    rows, columns, scale, info_ref, updates_ref, out_ref, grouped_ref, staged_ref, partial_ref
+):
     tile = pl.program_id(0)
 
     @pl.when(tile == 0)
     def _():
         if columns:
-            regroup(updates_ref, grouped_ref, rows, columns)
+            regroup(updates_ref, grouped_ref, staged_ref, rows, columns)
         else:
             grouped_ref[...] = updates_ref[...].astype(jnp.bfloat16)
 
@@ -136,26 +145,45 @@
     heights = row_heights(info_ref, rows)
     heights = [jnp.full((16, TILE), h, I32).astype(I16) for h in heights]
 
-    def add_block(block, total):
-        height, mixed, carry = column_terms(info_ref, lanes, block)
-        signs = []
-        for k in range(rows):
-            value = (((height + heights[k]) & I16(511)) - I16(256)) ^ mixed
-            value = value * short(8 * MUL_B) + carry
-            signs.append(jnp.where(value < 0, jnp.bfloat16(-1), jnp.bfloat16(1)))
+    blocks = grouped_ref.shape[0]
+    group = math.gcd(blocks, GROUP)
+
+    def add_group(index, total):
+        signs, updates = [], []
+        for member in range(group):
+            block = index * group + member
+            height, mixed, carry = column_terms(info_ref, lanes, block)
+            for k in range(rows):
+                value = (((height + heights[k]) & I16(511)) - I16(256)) ^ mixed
+                value = value * short(8 * MUL_B) + carry
+                signs.append(jnp.where(value < 0, jnp.bfloat16(-1), jnp.bfloat16(1)))
+            updates.append(grouped_ref[block])
         signs = jnp.concatenate(signs, 0)
-        return total + jnp.dot(grouped_ref[block], signs, preferred_element_type=jnp.float32)
-
-    out_ref[...] = lax.fori_loop(
-        0, grouped_ref.shape[0], add_block, jnp.zeros(out_ref.shape, jnp.float32)
-    )
-
-
-def project(info, updates):
+        updates = jnp.concatenate(updates, 1)
+        return total + jnp.dot(updates, signs, preferred_element_type=jnp.float32)
+
+    devices = out_ref.shape[0]
+    total = lax.fori_loop(
+        0, blocks // group, add_group, jnp.zeros((devices, TILE), jnp.float32)
+    )
+    here = pl.ds(pl.multiple_of(tile * devices, devices), devices)
+    for part in range(TILE // 128):
+        partial_ref[part, here, :] = total[:, part * 128 : part * 128 + 128] * scale
+
+    @pl.when(tile == FEAT // TILE - 1)
+    def _():
+        for device in range(devices):
+            for part in range(TILE // 128):
+                out_ref[device, :, part * 128 : part * 128 + 128] = partial_ref[
+                    part, pl.ds(device, FEAT // TILE, stride=devices), :
+                ].astype(jnp.bfloat16)
+
+
+def project(info, updates, scale):
     m, rows, columns = updates.shape
     blocks = columns // 16
     if rows % 8 == 0 and columns % 128 == 0:
-        flat = updates.reshape(m, rows * columns)
+        flat = updates.reshape(m * rows, columns)
         inside = columns
     else:
         flat = updates.reshape(m, rows, blocks, 16).transpose(2, 0, 1, 3)
@@ -163,14 +191,18 @@
         inside = 0
     whole = pl.BlockSpec(flat.shape, lambda t, i: (0,) * flat.ndim)
     return pl.pallas_call(
-        functools.partial(project_kernel, rows, inside),
-        out_shape=jax.ShapeDtypeStruct((m, FEAT), jnp.float32),
+        functools.partial(project_kernel, rows, inside, scale),
+        out_shape=jax.ShapeDtypeStruct((m, FEAT // TILE, TILE), jnp.bfloat16),
         grid_spec=pltpu.PrefetchScalarGridSpec(
             num_scalar_prefetch=1,
             grid=(FEAT // TILE,),
             in_specs=[whole],
-            out_specs=pl.BlockSpec((m, TILE), lambda t, i: (0, t)),
-            scratch_shapes=[pltpu.VMEM((blocks, m, rows * 16), jnp.bfloat16)],
+            out_specs=pl.BlockSpec((m, FEAT // TILE, TILE), lambda t, i: (0, 0, 0)),
+            scratch_shapes=[
+                pltpu.VMEM((blocks, m, rows * 16), jnp.bfloat16),
+                pltpu.VMEM((m * rows, 128), jnp.float32),
+                pltpu.VMEM((TILE // 128, FEAT // TILE * m, 128), jnp.float32),
+            ],
         ),
         name="project",
     )(info, flat)
@@ -191,15 +223,13 @@
     rank, inputs = down_matrix.shape
     rank_rows = 2 * rank
     rows, columns = rank_rows // holders, inputs // groups
-    devices = groups * holders
     params = rank_rows * inputs
     bound = acts.shape[1] * inputs * 6 * 0.125 * 0.5
     scale = 2.0 ** -max(0, math.ceil(math.log2(bound / 60000)))
     group, holder = lax.axis_index("wide"), lax.axis_index("narrow")
 
-    grads = sequence_grads(acts, cotangent, down_matrix, up_matrix, lengths)
-    sent = (grads * scale).astype(jnp.float16).reshape(holders, rows, groups, columns)
-    sent = sent.transpose(2, 0, 1, 3).reshape(devices, rows, columns)
+    grads = sequence_grads(groups, holders, acts, cotangent, down_matrix, up_matrix, lengths)
+    sent = (grads * scale).astype(jnp.float16)
     grads = lax.all_to_all(sent, AXES, 0, 0, tiled=True).astype(jnp.float32) * (1 / scale)
 
     def share(moment):
@@ -208,12 +238,12 @@
     first, second = share(adam_first_moment), share(adam_second_moment)
     moment_one = 0.9 * first[None] + 0.1 * grads
     moment_two = 0.999 * second[None] + 0.001 * grads * grads
-    updates = (moment_one / (jnp.sqrt(moment_two) + 1e-08)).astype(jnp.bfloat16)
+    updates = moment_one / (jnp.sqrt(moment_two) + 1e-08)
 
     info = jnp.stack([sign_hash_salt[0], holder * rows, group * columns])
-    partial = project(info, updates) * params**-0.5
-    parts = lax.all_to_all(partial.astype(jnp.float16), AXES, 0, 0, tiled=True)
-    return jnp.sum(parts.astype(jnp.float32), axis=0, keepdims=True)
+    partial = project(info, updates, params**-0.5)
+    parts = lax.all_to_all(partial, AXES, 0, 0, tiled=True)
+    return jnp.sum(parts.astype(jnp.float32), axis=0).reshape(1, FEAT)
 
 
 def solution(mesh):

time: 143 us -> 73.3 us (0.51)
  Pallas kernels: 95.3 us -> 31.4 us
  local copies, waits for them, and re-layouts: 6.4 us -> 1.55 us
    pallas_call x2, Pallas kernels: 95.3 us -> 31.4 us  [the longest x1 28.3 us: project(): pl.pallas_call(functools.partial(project_kernel, rows, inside, scale), ou...]
    unnamed x8 -> x5, local copies, waits for them, and re-layouts: 4.43 us -> 1.49 us
    all_to_all x2 -> x0, other arithmetic: 1.86 us -> none  [body(): parts = lax.all_to_all(partial.astype(jnp.float16), AXES, 0, 0, tiled=True)]
    div x0 -> x1, other arithmetic: none -> 1.56 us  [body(): updates = moment_one / (jnp.sqrt(moment_two) + 1e-08)]
where the time goes in v2:
time: 73.3 us; the launch traced here: 73 us
  Pallas kernels  31.4 us (43%)
  blocking collectives  13.6 us (19%)
  waiting for transfers between devices  13.3 us (18%)
  starting transfers between devices  7.32 us (10%)
  other arithmetic  4.43 us (6%)
  local copies, waits for them, and re-layouts  1.55 us (2%)
  between operations  1.35 us (2%)
    pallas_call x1, Pallas kernels, project(): pl.pallas_call(functools.partial(project_kernel, rows, inside, scale), ou...  28.3 us
    all_to_all x1, blocking collectives, body(): parts = lax.all_to_all(partial, AXES, 0, 0, tiled=True)  13.6 us
    all_to_all x1, waiting for transfers between devices, body(): lax.all_to_all(sent, AXES, 0, 0, tiled=True).astype(jnp.float32)  13.3 us
    all_to_all x1, starting transfers between devices, body(): lax.all_to_all(sent, AXES, 0, 0, tiled=True).astype(jnp.float32)  7.32 us
    pallas_call x1, Pallas kernels, sequence_grads(): pl.pallas_call(functools.partial(grads_kernel, holders), out_shape=jax.Sh...  3.06 us
    convert_element_type x1, other arithmetic, body(): sent = (grads * scale).astype(jnp.float16)  2.16 us
    div x1, other arithmetic, body(): updates = moment_one / (jnp.sqrt(moment_two) + 1e-08)  1.56 us
    unnamed x5, local copies, waits for them, and re-layouts  1.49 us
  transfers between devices with their start and end apart: 1, of which 1 were waited for; matrix products, arithmetic and copies ran while one was open for 1% of the time, Pallas kernels for 0%

profile of v2, /device:TPU:0, one launch (start us, length us, event | category | flops | bytes accessed | tf_op | source)
XLA Modules:
  0.0 73.0 jit_solution(9876376001360664964)
XLA Ops:
  0.7 3.1 %grads.1 = f32[32,16,512]{2,1,0:T(8,128)} custom-call(s32[1]{0:T(128)S(6)} %copy.10.length_ref, bf16[128,2048]{1,0:T(8,128)(2,1)} %bitcast.10, bf16[128,2048]{1,0:T(8,128)(2,1)} %bitcast.11, bf16[64,2048]{1,0:T(8,128)(2,1)} %down_ref.1, bf16[64,2048]{1,0:T(8,128)(2,1)} %bitcast.12), custom_call_target="tpu_custom_call" | custom-call | tf_op jit(solution)/shard_map/grads/pallas_call | solution.py:54
  3.7 2.2 %multiply_convert_fusion = f16[32,16,512]{2,1,0:T(8,128)(2,1)} fusion(f32[32,16,512]{2,1,0:T(8,128)} %grads.1), kind=kLoop, calls=%fused_computation.9 | loop fusion | flops 524288 | bytes 1572864 | tf_op jit(solution)/shard_map/convert_element_type | solution.py:232
  5.9 0.0 copy-start
  5.9 7.3 %all-to-all-start = ((f16[32,16,512]{2,1,0:T(8,128)(2,1)}), f16[32,16,512]{2,1,0:T(8,128)(2,1)S(1)}, u32[]{:S(2)}, u32[]{:S(2)}) async-start(f16[32,16,512]{2,1,0:T(8,128)(2,1)} %multiply_convert_fusion), calls=%async_computation | async-start | bytes 1048576 | tf_op jit(solution)/shard_map/all_to_all | solution.py:233
  13.9 0.0 copy-done
  13.9 0.0 copy-start.1
  13.9 0.9 %copy-done.1 = f32[32768]{0:T(1024)S(1)} copy-done((f32[32768]{0:T(1024)S(1)}, f32[32768]{0:T(1024)}, u32[]{:S(2)}) %copy-start.1) | copy-done | bytes 131096
  14.8 0.7 pad_add_fusion.info_ref
  15.5 13.3 %all-to-all-done = f16[32,16,512]{2,1,0:T(8,128)(2,1)S(1)} async-done(((f16[32,16,512]{2,1,0:T(8,128)(2,1)}), f16[32,16,512]{2,1,0:T(8,128)(2,1)S(1)}, u32[]{:S(2)}, u32[]{:S(2)}) %all-to-all-start) | async-done | bytes 524320 | tf_op jit(solution)/shard_map/all_to_all | solution.py:233
  28.8 1.6 %fusion.1 = f32[32,16,512]{2,1,0:T(8,128)} fusion(f16[32,16,512]{2,1,0:T(8,128)(2,1)S(1)} %all-to-all-done, f32[16,512]{1,0:T(8,128)S(1)} %get-tuple-element.5, f32[16,512]{1,0:T(8,128)S(1)} %get-tuple-element.6), kind=kLoop, calls=%fused_computation.4 | loop fusion | flops 2359296 | bytes 1638400 | tf_op jit(solution)/shard_map/div | solution.py:241
  30.4 28.3 %project.1 = bf16[32,8,512]{2,1,0:T(8,128)(2,1)} custom-call(s32[3]{0:T(128)} %pad_add_fusion.info_ref, f32[512,512]{1,0:T(8,128)} %bitcast.9), custom_call_target="tpu_custom_call" | custom-call | tf_op jit(solution)/shard_map/project/pallas_call | solution.py:193
  58.7 13.6 %all_to_all.10 = bf16[32,8,512]{2,1,0:T(8,128)(2,1)S(1)} all-to-all(bf16[32,8,512]{2,1,0:T(8,128)(2,1)} %project.1), channel_id=1, replica_groups=mesh['wide'=4,'narrow'=8] {'wide','narrow'}, dimensions={0} | all-to-all | bytes 524288 | tf_op jit(solution)/shard_map/all_to_all | solution.py:245
  72.3 0.6 copy.9
  (4 shorter events, 0.1 us)
Async XLA Ops:
  5.9 8.0 %copy-start = (f32[32768]{0:T(1024)S(1)}, f32[32768]{0:T(1024)}, u32[]{:S(2)}) copy-start(f32[32768]{0:T(1024)} %param.12) | copy-start | bytes 393220
  5.9 22.9 %all-to-all-start = ((f16[32,16,512]{2,1,0:T(8,128)(2,1)}), f16[32,16,512]{2,1,0:T(8,128)(2,1)S(1)}, u32[]{:S(2)}, u32[]{:S(2)}) async-start(f16[32,16,512]{2,1,0:T(8,128)(2,1)} %multiply_convert_fusion), calls=%async_computation | async-start | bytes 1048576 | tf_op jit(solution)/shard_map/all_to_all | solution.py:233
  13.9 0.9 %copy-start.1 = (f32[32768]{0:T(1024)S(1)}, f32[32768]{0:T(1024)}, u32[]{:S(2)}) copy-start(f32[32768]{0:T(1024)} %param.13) | copy-start | bytes 393220

commit v3 on v2

--- a/solution.py
+++ b/solution.py
@@ -16,9 +16,10 @@
 COLUMN_BITS = 11
 LOW = (1 << COLUMN_BITS) - 1
 TILE = 512
-GROUP = 32
+EARLY = 5
 I16 = jnp.int16
 I32 = jnp.int32
+SIGN = jnp.float8_e4m3fn
 
 
 def short(value):
@@ -60,8 +61,11 @@
     )(lengths, acts[0], cotangent[0], down_matrix, up_matrix.T)
 
 
-def lane_terms(info_ref, tile):
-    salt = info_ref[0]
+def position():
+    return lax.axis_index("wide"), lax.axis_index("narrow")
+
+
+def lane_terms(salt, tile):
     feature = lax.broadcasted_iota(I32, (8, TILE), 1) + tile * TILE
     product = (feature ^ (salt & (FEAT - 1))) * MUL_A + 1
     low = product & (FEAT - 1)
@@ -78,11 +82,10 @@
     )
 
 
-def column_terms(info_ref, lanes, block):
+def column_terms(salt, first, lanes):
     lane_low, lane_high, lane_top, lane_byte = lanes
-    salt_row = info_ref[0] >> 12
-    column = lax.broadcasted_iota(I32, (16, 128), 0) + (info_ref[2] + block * 16)
-    product = ((column ^ (salt_row & LOW)) * MUL_A) & 0xFFFFF
+    column = lax.broadcasted_iota(I32, (16, 128), 0) + first
+    product = ((column ^ ((salt >> 12) & LOW)) * MUL_A) & 0xFFFFF
     row_low = (product & LOW).astype(I16)
     row_high = (product >> COLUMN_BITS).astype(I16)
     wide = (1, TILE // 128)
@@ -98,15 +101,55 @@
     return height, mixed, carry
 
 
-def row_heights(info_ref, rows):
-    return [
-        (((info_ref[1] + k) ^ (info_ref[0] >> (12 + COLUMN_BITS))) * MUL_A) & 511
-        for k in range(rows)
-    ]
+def row_heights(salt, rows):
+    first = position()[1] * rows
+    heights = [(((first + k) ^ (salt >> (12 + COLUMN_BITS))) * MUL_A) & 511 for k in range(rows)]
+    return [jnp.full((16, TILE), h, I32).astype(I16) for h in heights]
+
+
+def block_signs(salt, columns, lanes, heights, block):
+    height, mixed, carry = column_terms(salt, position()[0] * columns + block * 16, lanes)
+    values = []
+    for row in heights:
+        value = (((height + row) & I16(511)) - I16(256)) ^ mixed
+        values.append(value * short(8 * MUL_B) + carry)
+    return jnp.where(jnp.concatenate(values, 0) < 0, SIGN(-1), SIGN(1))
+
+
+def signs_kernel(rows, columns, first_tile, salt_ref, after_ref, out_ref):
+    del after_ref
+    salt = salt_ref[0]
+    lanes = lane_terms(salt, pl.program_id(0) + first_tile)
+    heights = row_heights(salt, rows)
+    depth = 16 * rows
+
+    def store(block, _):
+        here = pl.ds(pl.multiple_of(block * depth, depth), depth)
+        out_ref[0, here, :] = block_signs(salt, columns, lanes, heights, block)
+        return 0
+
+    lax.fori_loop(0, columns // 16, store, 0, unroll=2)
+
+
+def early_signs(salt, rows, columns, after):
+    return pl.pallas_call(
+        functools.partial(signs_kernel, rows, columns, FEAT // TILE - EARLY),
+        out_shape=jax.ShapeDtypeStruct((EARLY, rows * columns, TILE), SIGN),
+        grid_spec=pltpu.PrefetchScalarGridSpec(
+            num_scalar_prefetch=1,
+            grid=(EARLY,),
+            in_specs=[pl.BlockSpec(memory_space=pl.ANY)],
+            out_specs=pl.BlockSpec((1, rows * columns, TILE), lambda t, i: (t, 0, 0)),
+        ),
+        cost_estimate=pl.CostEstimate(
+            flops=EARLY * rows * columns * TILE * 256, bytes_accessed=0, transcendentals=0
+        ),
+        name="early_signs",
+    )(salt, after)
 
 
 def regroup(updates_ref, grouped_ref, staged_ref, rows, columns):
-    devices = grouped_ref.shape[1]
+    devices = grouped_ref.shape[0]
     lane = lax.broadcasted_iota(I32, (devices, 128), 1)
     for part in range(columns // 128):
         staged_ref[...] = updates_ref[:, part * 128 : part * 128 + 128]
@@ -124,88 +167,102 @@
                     pieces[k] = jnp.where(upper, pltpu.roll(b, 16 * step, 1), a)
                     pieces[k + step] = jnp.where(upper, b, pltpu.roll(a, 128 - 16 * step, 1))
             for c in range(8):
-                grouped_ref[part * 8 + c, :, half * 128 : half * 128 + 128] = pieces[c].astype(
-                    jnp.bfloat16
-                )
+                start = ((part * 8 + c) * rows + half * 8) * 16
+                grouped_ref[:, start : start + 128] = pieces[c].astype(jnp.bfloat16)
 
 
 def project_kernel(
-    rows, columns, scale, info_ref, updates_ref, out_ref, grouped_ref, staged_ref, partial_ref
+    rows,
+    columns,
+    scale,
+    salt_ref,
+    updates_ref,
+    early_ref,
+    out_ref,
+    grouped_ref,
+    staged_ref,
+    partial_ref,
+    signs_ref,
+    sems,
 ):
     tile = pl.program_id(0)
+    tiles = FEAT // TILE
+    devices = out_ref.shape[0]
+    depth = 16 * rows
+
+    def fetch(index):
+        return pltpu.make_async_copy(early_ref.at[index], signs_ref.at[index], sems.at[index])
 
     @pl.when(tile == 0)
     def _():
-        if columns:
+        for index in range(EARLY):
+            fetch(index).start()
+        if staged_ref.shape[0] > 8:
             regroup(updates_ref, grouped_ref, staged_ref, rows, columns)
         else:
             grouped_ref[...] = updates_ref[...].astype(jnp.bfloat16)
 
-    lanes = lane_terms(info_ref, tile)
-    heights = row_heights(info_ref, rows)
-    heights = [jnp.full((16, TILE), h, I32).astype(I16) for h in heights]
-
-    blocks = grouped_ref.shape[0]
-    group = math.gcd(blocks, GROUP)
-
-    def add_group(index, total):
-        signs, updates = [], []
-        for member in range(group):
-            block = index * group + member
-            height, mixed, carry = column_terms(info_ref, lanes, block)
-            for k in range(rows):
-                value = (((height + heights[k]) & I16(511)) - I16(256)) ^ mixed
-                value = value * short(8 * MUL_B) + carry
-                signs.append(jnp.where(value < 0, jnp.bfloat16(-1), jnp.bfloat16(1)))
-            updates.append(grouped_ref[block])
+    def finish(total):
+        here = pl.ds(pl.multiple_of(tile * devices, devices), devices)
+        for part in range(TILE // 128):
+            partial_ref[part, here, :] = total[:, part * 128 : part * 128 + 128] * scale
+
+    @pl.when(tile < tiles - EARLY)
+    def _():
+        salt = salt_ref[0]
+        lanes = lane_terms(salt, tile)
+        heights = row_heights(salt, rows)
+        signs = [
+            block_signs(salt, columns, lanes, heights, block) for block in range(columns // 16)
+        ]
         signs = jnp.concatenate(signs, 0)
-        updates = jnp.concatenate(updates, 1)
-        return total + jnp.dot(updates, signs, preferred_element_type=jnp.float32)
-
-    devices = out_ref.shape[0]
-    total = lax.fori_loop(
-        0, blocks // group, add_group, jnp.zeros((devices, TILE), jnp.float32)
-    )
-    here = pl.ds(pl.multiple_of(tile * devices, devices), devices)
-    for part in range(TILE // 128):
-        partial_ref[part, here, :] = total[:, part * 128 : part * 128 + 128] * scale
-
-    @pl.when(tile == FEAT // TILE - 1)
+        finish(jnp.dot(grouped_ref[...], signs, preferred_element_type=jnp.float32))
+
+    @pl.when(tile >= tiles - EARLY)
+    def _():
+        index = tile - (tiles - EARLY)
+        fetch(index).wait()
+        finish(jnp.dot(grouped_ref[...], signs_ref[index], preferred_element_type=jnp.float32))
+
+    @pl.when(tile == tiles - 1)
     def _():
         for device in range(devices):
             for part in range(TILE // 128):
                 out_ref[device, :, part * 128 : part * 128 + 128] = partial_ref[
-                    part, pl.ds(device, FEAT // TILE, stride=devices), :
+                    part, pl.ds(device, tiles, stride=devices), :
                 ].astype(jnp.bfloat16)
 
 
-def project(info, updates, scale):
+def project(salt, updates, early, scale):
     m, rows, columns = updates.shape
-    blocks = columns // 16
     if rows % 8 == 0 and columns % 128 == 0:
         flat = updates.reshape(m * rows, columns)
-        inside = columns
+        staged = m * rows
     else:
-        flat = updates.reshape(m, rows, blocks, 16).transpose(2, 0, 1, 3)
-        flat = flat.reshape(blocks, m, rows * 16)
-        inside = 0
-    whole = pl.BlockSpec(flat.shape, lambda t, i: (0,) * flat.ndim)
+        flat = updates.reshape(m, rows, columns // 16, 16).transpose(0, 2, 1, 3)
+        flat = flat.reshape(m, rows * columns)
+        staged = 8
     return pl.pallas_call(
-        functools.partial(project_kernel, rows, inside, scale),
+        functools.partial(project_kernel, rows, columns, scale),
         out_shape=jax.ShapeDtypeStruct((m, FEAT // TILE, TILE), jnp.bfloat16),
         grid_spec=pltpu.PrefetchScalarGridSpec(
             num_scalar_prefetch=1,
             grid=(FEAT // TILE,),
-            in_specs=[whole],
+            in_specs=[
+                pl.BlockSpec(flat.shape, lambda t, i: (0, 0)),
+                pl.BlockSpec(memory_space=pl.ANY),
+            ],
             out_specs=pl.BlockSpec((m, FEAT // TILE, TILE), lambda t, i: (0, 0, 0)),
             scratch_shapes=[
-                pltpu.VMEM((blocks, m, rows * 16), jnp.bfloat16),
-                pltpu.VMEM((m * rows, 128), jnp.float32),
+                pltpu.VMEM((m, rows * columns), jnp.bfloat16),
+                pltpu.VMEM((staged, 128), jnp.float32),
                 pltpu.VMEM((TILE // 128, FEAT // TILE * m, 128), jnp.float32),
+                pltpu.VMEM((EARLY, rows * columns, TILE), SIGN),
+                pltpu.SemaphoreType.DMA((EARLY,)),
             ],
         ),
         name="project",
-    )(info, flat)
+    )(salt, flat, early)
 
 
 def body(
@@ -226,10 +283,11 @@
     params = rank_rows * inputs
     bound = acts.shape[1] * inputs * 6 * 0.125 * 0.5
     scale = 2.0 ** -max(0, math.ceil(math.log2(bound / 60000)))
-    group, holder = lax.axis_index("wide"), lax.axis_index("narrow")
-
-    grads = sequence_grads(groups, holders, acts, cotangent, down_matrix, up_matrix, lengths)
-    sent = (grads * scale).astype(jnp.float16)
+    group = lax.axis_index("wide")
+
+    slabs = sequence_grads(groups, holders, acts, cotangent, down_matrix, up_matrix, lengths)
+    sent = (slabs * scale).astype(jnp.float16)
+    early = early_signs(sign_hash_salt, rows, columns, slabs)
     grads = lax.all_to_all(sent, AXES, 0, 0, tiled=True).astype(jnp.float32) * (1 / scale)
 
     def share(moment):
@@ -240,8 +298,7 @@
     moment_two = 0.999 * second[None] + 0.001 * grads * grads
     updates = moment_one / (jnp.sqrt(moment_two) + 1e-08)
 
-    info = jnp.stack([sign_hash_salt[0], holder * rows, group * columns])
-    partial = project(info, updates, params**-0.5)
+    partial = project(sign_hash_salt, updates, early, params**-0.5)
     parts = lax.all_to_all(partial, AXES, 0, 0, tiled=True)
     return jnp.sum(parts.astype(jnp.float32), axis=0).reshape(1, FEAT)
 

time: 73.3 us -> 65.1 us (0.89)
  waiting for transfers between devices: 13.3 us -> 0.01 us
  blocking collectives: 13.6 us -> 16.4 us
  Pallas kernels: 31.4 us -> 33.4 us
  local copies, waits for them, and re-layouts: 1.55 us -> 2.49 us
    all_to_all x1, waiting for transfers between devices: 13.3 us -> 0.01 us  [body(): lax.all_to_all(sent, AXES, 0, 0, tiled=True).astype(jnp.float32)]
    all_to_all x1, blocking collectives: 13.6 us -> 16.4 us  [body(): parts = lax.all_to_all(partial, AXES, 0, 0, tiled=True)]
    pallas_call x1 -> x2, Pallas kernels: 28.3 us -> 30.3 us  [the longest x1 15.4 us: early_signs(): pl.pallas_call(functools.partial(signs_kernel, rows, columns, FEAT // TIL...]
    reshape x2, local copies, waits for them, and re-layouts: 0.06 us -> 1.87 us  [share(): moment.reshape(rows, inputs)]
    unnamed x5 -> x1, local copies, waits for them, and re-layouts: 1.49 us -> 0.62 us
  transfers between devices with their start and end apart: 1 -> 1, of which waited for: 1 -> 0; matrix products, arithmetic and copies ran while one was open for 1% -> 3% of each run, Pallas kernels for 0% -> 24%
where the time goes in v3:
time: 65.1 us; the launch traced here: 64.7 us
  Pallas kernels  33.4 us (51%)
  blocking collectives  16.4 us (25%)
  starting transfers between devices  7.32 us (11%)
  other arithmetic  3.79 us (6%)
  local copies, waits for them, and re-layouts  2.49 us (4%)
  between operations  1.34 us (2%)
    all_to_all x1, blocking collectives, body(): parts = lax.all_to_all(partial, AXES, 0, 0, tiled=True)  16.4 us
    pallas_call x1, Pallas kernels, early_signs(): pl.pallas_call(functools.partial(signs_kernel, rows, columns, FEAT // TIL...  15.4 us
    pallas_call x1, Pallas kernels, project(): pl.pallas_call(functools.partial(project_kernel, rows, columns, scale), o...  14.9 us
    all_to_all x1, starting transfers between devices, body(): lax.all_to_all(sent, AXES, 0, 0, tiled=True).astype(jnp.float32)  7.32 us
    pallas_call x1, Pallas kernels, sequence_grads(): pl.pallas_call(functools.partial(grads_kernel, holders), out_shape=jax.Sh...  3.06 us
    convert_element_type x1, other arithmetic, body(): sent = (slabs * scale).astype(jnp.float16)  2.17 us
    reshape x2, local copies, waits for them, and re-layouts, share(): moment.reshape(rows, inputs)  1.87 us
    div x1, other arithmetic, body(): updates = moment_one / (jnp.sqrt(moment_two) + 1e-08)  1.56 us
  transfers between devices with their start and end apart: 1, of which 0 were waited for; matrix products, arithmetic and copies ran while one was open for 3% of the time, Pallas kernels for 24%

profile of v3, /device:TPU:0, one launch (start us, length us, event | category | flops | bytes accessed | tf_op | source)
XLA Modules:
  0.0 64.7 jit_solution(14895018131809631453)
XLA Ops:
  0.7 3.1 %grads.1.after_ref = f32[32,16,512]{2,1,0:T(8,128)} custom-call(s32[1]{0:T(128)S(6)} %copy.10.length_ref, bf16[128,2048]{1,0:T(8,128)(2,1)} %bitcast.8, bf16[128,2048]{1,0:T(8,128)(2,1)} %bitcast.9, bf16[64,2048]{1,0:T(8,128)(2,1)} %down_ref.1, bf16[64,2048]{1,0:T(8,128)(2,1)} %bitcast.10), custom_call_target="tpu_custom_call" | custom-call | tf_op jit(solution)/shard_map/grads/pallas_call | solution.py:55
  3.7 2.2 %multiply_convert_fusion = f16[32,16,512]{2,1,0:T(8,128)(2,1)} fusion(f32[32,16,512]{2,1,0:T(8,128)} %grads.1.after_ref), kind=kLoop, calls=%fused_computation.9 | loop fusion | flops 524288 | bytes 1572864 | tf_op jit(solution)/shard_map/convert_element_type | solution.py:289
  5.9 7.3 %all-to-all-start = ((f16[32,16,512]{2,1,0:T(8,128)(2,1)}), f16[32,16,512]{2,1,0:T(8,128)(2,1)S(1)}, u32[]{:S(2)}, u32[]{:S(2)}) async-start(f16[32,16,512]{2,1,0:T(8,128)(2,1)} %multiply_convert_fusion), calls=%async_computation | async-start | bytes 1048576 | tf_op jit(solution)/shard_map/all_to_all | solution.py:291
  13.9 0.9 %reshape.16 = f32[16,2048]{1,0:T(8,128)S(1)} reshape(f32[32768]{0:T(1024)} %param.12) | data formatting | bytes 262144 | tf_op jit(solution)/shard_map/reshape | solution.py:294
  14.8 0.9 %reshape.17 = f32[16,2048]{1,0:T(8,128)S(1)} reshape(f32[32768]{0:T(1024)} %param.13) | data formatting | bytes 262144 | tf_op jit(solution)/shard_map/reshape | solution.py:294
  15.8 15.4 %early_signs.1.early_ref = f8e4m3fn[5,8192,512]{2,1,0:T(32,128)(4,1)} custom-call(s32[1]{0:T(128)S(6)} %copy.11.salt_ref, f32[32,16,512]{2,1,0:T(8,128)} %grads.1.after_ref), custom_call_target="tpu_custom_call" | custom-call | flops 5368709120 | tf_op jit(solution)/shard_map/early_signs/pallas_call | solution.py:135
  31.1 0.0 all-to-all-done
  31.1 1.6 %fusion.1 = f32[32,16,512]{2,1,0:T(8,128)} fusion(f16[32,16,512]{2,1,0:T(8,128)(2,1)S(1)} %all-to-all-done, f32[16,512]{1,0:T(8,128)S(1)} %get-tuple-element.5, f32[16,512]{1,0:T(8,128)S(1)} %get-tuple-element.6), kind=kLoop, calls=%fused_computation.4 | loop fusion | flops 2359296 | bytes 1638400 | tf_op jit(solution)/shard_map/div | solution.py:299
  32.7 14.9 %project.1 = bf16[32,8,512]{2,1,0:T(8,128)(2,1)} custom-call(s32[1]{0:T(128)S(6)} %copy.11.salt_ref, f32[512,512]{1,0:T(8,128)} %bitcast.7, f8e4m3fn[5,8192,512]{2,1,0:T(32,128)(4,1)} %early_signs.1.early_ref), custom_call_target="tpu_custom_call" | custom-call | tf_op jit(solution)/shard_map/project/pallas_call | solution.py:245
  47.6 16.4 %all_to_all.10 = bf16[32,8,512]{2,1,0:T(8,128)(2,1)S(1)} all-to-all(bf16[32,8,512]{2,1,0:T(8,128)(2,1)} %project.1), channel_id=1, replica_groups=mesh['wide'=4,'narrow'=8] {'wide','narrow'}, dimensions={0} | all-to-all | bytes 524288 | tf_op jit(solution)/shard_map/all_to_all | solution.py:302
  64.1 0.6 copy.9
  (2 shorter events, 0.1 us)
Async XLA Ops:
  5.9 25.2 %all-to-all-start = ((f16[32,16,512]{2,1,0:T(8,128)(2,1)}), f16[32,16,512]{2,1,0:T(8,128)(2,1)S(1)}, u32[]{:S(2)}, u32[]{:S(2)}) async-start(f16[32,16,512]{2,1,0:T(8,128)(2,1)} %multiply_convert_fusion), calls=%async_computation | async-start | bytes 1048576 | tf_op jit(solution)/shard_map/all_to_all | solution.py:291

commit v4 on v3

--- a/solution.py
+++ b/solution.py
@@ -16,6 +16,7 @@
 COLUMN_BITS = 11
 LOW = (1 << COLUMN_BITS) - 1
 TILE = 512
+GROUP = 2
 EARLY = 5
 I16 = jnp.int16
 I32 = jnp.int32
@@ -116,13 +117,23 @@
     return jnp.where(jnp.concatenate(values, 0) < 0, SIGN(-1), SIGN(1))
 
 
-def signs_kernel(rows, columns, first_tile, salt_ref, after_ref, out_ref):
+def signs_kernel(
+    rows, columns, first_tile, salt_ref, after_ref, first_ref, second_ref, out_ref, one_ref, two_ref
+):
     del after_ref
     salt = salt_ref[0]
     lanes = lane_terms(salt, pl.program_id(0) + first_tile)
     heights = row_heights(salt, rows)
     depth = 16 * rows
 
+    @pl.when(pl.program_id(0) == 0)
+    def _():
+        stride = first_ref.shape[0] // rows
+        for part in range(columns // 128):
+            here = pl.ds(position()[0] * (columns // 128) + part, rows, stride=stride)
+            one_ref[:, part * 128 : part * 128 + 128] = first_ref[here, :]
+            two_ref[:, part * 128 : part * 128 + 128] = second_ref[here, :]
+
     def store(block, _):
         here = pl.ds(pl.multiple_of(block * depth, depth), depth)
         out_ref[0, here, :] = block_signs(salt, columns, lanes, heights, block)
@@ -131,21 +142,32 @@
     lax.fori_loop(0, columns // 16, store, 0, unroll=2)
 
 
-def early_signs(salt, rows, columns, after):
+def early_signs(salt, rows, columns, after, first, second):
+    whole = pl.BlockSpec((first.size // 128, 128), lambda t, i: (0, 0))
+    share = pl.BlockSpec((rows, columns), lambda t, i: (0, 0))
+    moment = jax.ShapeDtypeStruct((rows, columns), jnp.float32)
     return pl.pallas_call(
         functools.partial(signs_kernel, rows, columns, FEAT // TILE - EARLY),
-        out_shape=jax.ShapeDtypeStruct((EARLY, rows * columns, TILE), SIGN),
+        out_shape=(
+            jax.ShapeDtypeStruct((EARLY, rows * columns, TILE), SIGN),
+            moment,
+            moment,
+        ),
         grid_spec=pltpu.PrefetchScalarGridSpec(
             num_scalar_prefetch=1,
             grid=(EARLY,),
-            in_specs=[pl.BlockSpec(memory_space=pl.ANY)],
-            out_specs=pl.BlockSpec((1, rows * columns, TILE), lambda t, i: (t, 0, 0)),
+            in_specs=[pl.BlockSpec(memory_space=pl.ANY), whole, whole],
+            out_specs=(
+                pl.BlockSpec((1, rows * columns, TILE), lambda t, i: (t, 0, 0)),
+                share,
+                share,
+            ),
         ),
         cost_estimate=pl.CostEstimate(
             flops=EARLY * rows * columns * TILE * 256, bytes_accessed=0, transcendentals=0
         ),
         name="early_signs",
-    )(salt, after)
+    )(salt, after, first.reshape(-1, 128), second.reshape(-1, 128))
 
 
 def regroup(updates_ref, grouped_ref, staged_ref, rows, columns):
@@ -185,52 +207,59 @@
     signs_ref,
     sems,
 ):
-    tile = pl.program_id(0)
-    tiles = FEAT // TILE
     devices = out_ref.shape[0]
-    depth = 16 * rows
+    late = FEAT // TILE - EARLY
 
     def fetch(index):
         return pltpu.make_async_copy(early_ref.at[index], signs_ref.at[index], sems.at[index])
 
-    @pl.when(tile == 0)
-    def _():
-        for index in range(EARLY):
-            fetch(index).start()
-        if staged_ref.shape[0] > 8:
-            regroup(updates_ref, grouped_ref, staged_ref, rows, columns)
-        else:
-            grouped_ref[...] = updates_ref[...].astype(jnp.bfloat16)
-
-    def finish(total):
-        here = pl.ds(pl.multiple_of(tile * devices, devices), devices)
+    def product(start, signs):
+        updates = grouped_ref[:, start : start + signs.shape[0]]
+        return jnp.dot(updates, signs, preferred_element_type=jnp.float32)
+
+    def finish(tile, total):
+        total = total * scale
         for part in range(TILE // 128):
-            partial_ref[part, here, :] = total[:, part * 128 : part * 128 + 128] * scale
-
-    @pl.when(tile < tiles - EARLY)
-    def _():
-        salt = salt_ref[0]
+            start = (tile * (TILE // 128) + part) * devices
+            partial_ref[start : start + devices, :] = total[:, part * 128 : part * 128 + 128]
+
+    for index in range(EARLY):
+        fetch(index).start()
+    if staged_ref.shape[0] > 8:
+        regroup(updates_ref, grouped_ref, staged_ref, rows, columns)
+    else:
+        grouped_ref[...] = updates_ref[...].astype(jnp.bfloat16)
+
+    salt = salt_ref[0]
+    heights = row_heights(salt, rows)
+    done = 0
+    for tile in range(late):
+        ready = EARLY * tile // max(late - 1, 1)
+        for index in range(done, ready):
+            fetch(index).wait()
         lanes = lane_terms(salt, tile)
-        heights = row_heights(salt, rows)
-        signs = [
-            block_signs(salt, columns, lanes, heights, block) for block in range(columns // 16)
-        ]
-        signs = jnp.concatenate(signs, 0)
-        finish(jnp.dot(grouped_ref[...], signs, preferred_element_type=jnp.float32))
-
-    @pl.when(tile >= tiles - EARLY)
-    def _():
-        index = tile - (tiles - EARLY)
-        fetch(index).wait()
-        finish(jnp.dot(grouped_ref[...], signs_ref[index], preferred_element_type=jnp.float32))
-
-    @pl.when(tile == tiles - 1)
-    def _():
-        for device in range(devices):
-            for part in range(TILE // 128):
-                out_ref[device, :, part * 128 : part * 128 + 128] = partial_ref[
-                    part, pl.ds(device, tiles, stride=devices), :
-                ].astype(jnp.bfloat16)
+        totals = [0.0] * (1 + ready - done)
+        blocks = columns // 16
+        group = math.gcd(blocks, GROUP)
+        for block in range(0, blocks, group):
+            start, size = block * rows * 16, group * rows * 16
+            for index in range(done, ready):
+                stored = signs_ref[index, start : start + size, :]
+                totals[1 + index - done] += product(start, stored)
+            signs = [
+                block_signs(salt, columns, lanes, heights, block + member)
+                for member in range(group)
+            ]
+            totals[0] += product(start, jnp.concatenate(signs, 0))
+        finish(tile, totals[0])
+        for index in range(done, ready):
+            finish(late + index, totals[1 + index - done])
+        done = ready
+
+    for device in range(devices):
+        out_ref[device] = partial_ref[
+            pl.ds(device, FEAT // 128, stride=devices), :
+        ].astype(jnp.bfloat16)
 
 
 def project(salt, updates, early, scale):
@@ -244,23 +273,20 @@
         staged = 8
     return pl.pallas_call(
         functools.partial(project_kernel, rows, columns, scale),
-        out_shape=jax.ShapeDtypeStruct((m, FEAT // TILE, TILE), jnp.bfloat16),
-        grid_spec=pltpu.PrefetchScalarGridSpec(
-            num_scalar_prefetch=1,
-            grid=(FEAT // TILE,),
-            in_specs=[
-                pl.BlockSpec(flat.shape, lambda t, i: (0, 0)),
-                pl.BlockSpec(memory_space=pl.ANY),
-            ],
-            out_specs=pl.BlockSpec((m, FEAT // TILE, TILE), lambda t, i: (0, 0, 0)),
-            scratch_shapes=[
-                pltpu.VMEM((m, rows * columns), jnp.bfloat16),
-                pltpu.VMEM((staged, 128), jnp.float32),
-                pltpu.VMEM((TILE // 128, FEAT // TILE * m, 128), jnp.float32),
-                pltpu.VMEM((EARLY, rows * columns, TILE), SIGN),
-                pltpu.SemaphoreType.DMA((EARLY,)),
-            ],
-        ),
+        out_shape=jax.ShapeDtypeStruct((m, FEAT // 128, 128), jnp.bfloat16),
+        in_specs=[
+            pl.BlockSpec(memory_space=pltpu.SMEM),
+            pl.BlockSpec(memory_space=pltpu.VMEM),
+            pl.BlockSpec(memory_space=pl.ANY),
+        ],
+        out_specs=pl.BlockSpec(memory_space=pltpu.VMEM),
+        scratch_shapes=[
+            pltpu.VMEM((m, rows * columns), jnp.bfloat16),
+            pltpu.VMEM((staged, 128), jnp.float32),
+            pltpu.VMEM((FEAT // 128 * m, 128), jnp.float32),
+            pltpu.VMEM((EARLY, rows * columns, TILE), SIGN),
+            pltpu.SemaphoreType.DMA((EARLY,)),
+        ],
         name="project",
     )(salt, flat, early)
 
@@ -283,17 +309,14 @@
     params = rank_rows * inputs
     bound = acts.shape[1] * inputs * 6 * 0.125 * 0.5
     scale = 2.0 ** -max(0, math.ceil(math.log2(bound / 60000)))
-    group = lax.axis_index("wide")
 
     slabs = sequence_grads(groups, holders, acts, cotangent, down_matrix, up_matrix, lengths)
     sent = (slabs * scale).astype(jnp.float16)
-    early = early_signs(sign_hash_salt, rows, columns, slabs)
+    early, first, second = early_signs(
+        sign_hash_salt, rows, columns, slabs, adam_first_moment, adam_second_moment
+    )
     grads = lax.all_to_all(sent, AXES, 0, 0, tiled=True).astype(jnp.float32) * (1 / scale)
 
-    def share(moment):
-        return lax.dynamic_slice_in_dim(moment.reshape(rows, inputs), group * columns, columns, 1)
-
-    first, second = share(adam_first_moment), share(adam_second_moment)
     moment_one = 0.9 * first[None] + 0.1 * grads
     moment_two = 0.999 * second[None] + 0.001 * grads * grads
     updates = moment_one / (jnp.sqrt(moment_two) + 1e-08)

time: 65.1 us -> 65.6 us (level)
  local copies, waits for them, and re-layouts: 2.49 us -> 0 us
  Pallas kernels: 33.4 us -> 34.9 us
  other arithmetic: 3.79 us -> 5.17 us
    reshape x2 -> x0, local copies, waits for them, and re-layouts: 1.87 us -> none  [share(): moment.reshape(rows, inputs)]
    pallas_call x1, Pallas kernels: 15.4 us -> 16.4 us  [early_signs(): pl.pallas_call(functools.partial(signs_kernel, rows, columns, FEAT // TIL...]
    mul x1, other arithmetic: 0.02 us -> 0.78 us  [body(): moment_two = 0.999 * second[None] + 0.001 * grads * grads]
  transfers between devices with their start and end apart: 1 -> 1, of which waited for: 0 -> 0; matrix products, arithmetic and copies ran while one was open for 3% -> 1% of each run, Pallas kernels for 24% -> 25%
where the time goes in v4:
time: 65.6 us; the launch traced here: 65.2 us
  Pallas kernels  34.9 us (53%)
  blocking collectives  16.4 us (25%)
  starting transfers between devices  7.32 us (11%)
  other arithmetic  5.17 us (8%)
  between operations  1.32 us (2%)
    pallas_call x1, Pallas kernels, early_signs(): pl.pallas_call(functools.partial(signs_kernel, rows, columns, FEAT // TIL...  16.4 us
    all_to_all x1, blocking collectives, body(): parts = lax.all_to_all(partial, AXES, 0, 0, tiled=True)  16.4 us
    pallas_call x1, Pallas kernels, project(): pl.pallas_call(functools.partial(project_kernel, rows, columns, scale), o...  15.4 us
    all_to_all x1, starting transfers between devices, body(): lax.all_to_all(sent, AXES, 0, 0, tiled=True).astype(jnp.float32)  7.32 us
    pallas_call x1, Pallas kernels, sequence_grads(): pl.pallas_call(functools.partial(grads_kernel, holders), out_shape=jax.Sh...  3.06 us
    convert_element_type x1, other arithmetic, body(): sent = (slabs * scale).astype(jnp.float16)  2.18 us
    div x1, other arithmetic, body(): updates = moment_one / (jnp.sqrt(moment_two) + 1e-08)  1.55 us
  transfers between devices with their start and end apart: 1, of which 0 were waited for; matrix products, arithmetic and copies ran while one was open for 1% of the time, Pallas kernels for 25%

profile of v4, /device:TPU:0, one launch (start us, length us, event | category | flops | bytes accessed | tf_op | source)
XLA Modules:
  0.0 65.2 jit_solution(85580761127762189)
XLA Ops:
  0.7 3.1 %grads.1.after_ref = f32[32,16,512]{2,1,0:T(8,128)} custom-call(s32[1]{0:T(128)S(6)} %copy.9.length_ref, bf16[128,2048]{1,0:T(8,128)(2,1)} %bitcast.8, bf16[128,2048]{1,0:T(8,128)(2,1)} %bitcast.9, bf16[64,2048]{1,0:T(8,128)(2,1)} %down_ref.1, bf16[64,2048]{1,0:T(8,128)(2,1)} %bitcast.10), custom_call_target="tpu_custom_call" | custom-call | tf_op jit(solution)/shard_map/grads/pallas_call | solution.py:56
  3.7 2.2 %multiply_convert_fusion = f16[32,16,512]{2,1,0:T(8,128)(2,1)} fusion(f32[32,16,512]{2,1,0:T(8,128)} %grads.1.after_ref), kind=kLoop, calls=%fused_computation.9 | loop fusion | flops 524288 | bytes 1572864 | tf_op jit(solution)/shard_map/convert_element_type | solution.py:314
  5.9 7.3 %all-to-all-start = ((f16[32,16,512]{2,1,0:T(8,128)(2,1)}), f16[32,16,512]{2,1,0:T(8,128)(2,1)S(1)}, u32[]{:S(2)}, u32[]{:S(2)}) async-start(f16[32,16,512]{2,1,0:T(8,128)(2,1)} %multiply_convert_fusion), calls=%async_computation | async-start | bytes 1048576 | tf_op jit(solution)/shard_map/all_to_all | solution.py:318
  13.9 16.4 %early_signs.1 = (f8e4m3fn[5,8192,512]{2,1,0:T(32,128)(4,1)}, f32[16,512]{1,0:T(8,128)}, f32[16,512]{1,0:T(8,128)}) custom-call(s32[1]{0:T(128)S(6)} %copy.10.salt_ref, f32[32,16,512]{2,1,0:T(8,128)} %grads.1.after_ref, f32[256,128]{1,0:T(8,128)} %bitcast.11, f32[256,128]{1,0:T(8,128)} %bitcast.12), custom_call_target="tpu_custom_call" | custom-call | flops 5368709120 | tf_op jit(solution)/shard_map/early_signs/pallas_call | solution.py:149
  30.3 0.8 %broadcast_multiply_fusion = (f32[16,512]{1,0:T(8,128)S(1)}, f32[16,512]{1,0:T(8,128)S(1)}) fusion(f32[16,512]{1,0:T(8,128)} %get-tuple-element.9, f32[16,512]{1,0:T(8,128)} %get-tuple-element.8), kind=kLoop, calls=%fused_computation.11 | loop fusion | flops 16384 | bytes 131072 | tf_op jit(solution)/shard_map/mul | solution.py:321
  31.1 0.0 all-to-all-done
  31.1 1.6 %fusion.1 = f32[32,16,512]{2,1,0:T(8,128)} fusion(f16[32,16,512]{2,1,0:T(8,128)(2,1)S(1)} %all-to-all-done, f32[16,512]{1,0:T(8,128)S(1)} %get-tuple-element.11, f32[16,512]{1,0:T(8,128)S(1)} %get-tuple-element.12), kind=kLoop, calls=%fused_computation.4 | loop fusion | flops 2359296 | bytes 1638400 | tf_op jit(solution)/shard_map/div | solution.py:322
  32.7 15.4 %project.1 = bf16[32,32,128]{2,1,0:T(8,128)(2,1)} custom-call(s32[1]{0:T(128)S(6)} %copy.10.salt_ref, f32[512,512]{1,0:T(8,128)} %bitcast.7, f8e4m3fn[5,8192,512]{2,1,0:T(32,128)(4,1)} %get-tuple-element.10.early_ref), custom_call_target="tpu_custom_call" | custom-call | tf_op jit(solution)/shard_map/project/pallas_call | solution.py:274
  48.1 16.4 %all_to_all.10 = bf16[32,32,128]{2,1,0:T(8,128)(2,1)S(1)} all-to-all(bf16[32,32,128]{2,1,0:T(8,128)(2,1)} %project.1), channel_id=1, replica_groups=mesh['wide'=4,'narrow'=8] {'wide','narrow'}, dimensions={0} | all-to-all | bytes 524288 | tf_op jit(solution)/shard_map/all_to_all | solution.py:325
  64.5 0.7 convert_reduce_fusion
Async XLA Ops:
  5.9 25.2 %all-to-all-start = ((f16[32,16,512]{2,1,0:T(8,128)(2,1)}), f16[32,16,512]{2,1,0:T(8,128)(2,1)S(1)}, u32[]{:S(2)}, u32[]{:S(2)}) async-start(f16[32,16,512]{2,1,0:T(8,128)(2,1)} %multiply_convert_fusion), calls=%async_computation | async-start | bytes 1048576 | tf_op jit(solution)/shard_map/all_to_all | solution.py:318

commit v5 on v4

--- a/solution.py
+++ b/solution.py
@@ -17,6 +17,7 @@
 LOW = (1 << COLUMN_BITS) - 1
 TILE = 512
 GROUP = 2
+AHEAD = 2
 EARLY = 5
 I16 = jnp.int16
 I32 = jnp.int32
@@ -46,7 +47,7 @@
             for group in range(groups):
                 grads_ref[group * holders + half * (holders // 2) + holder] = grads[
                     holder * rows : (holder + 1) * rows, group * columns : (group + 1) * columns
-                ]
+                ].astype(jnp.bfloat16)
 
 
 def sequence_grads(groups, holders, acts, cotangent, down_matrix, up_matrix, lengths):
@@ -55,7 +56,7 @@
     slabs = (groups * holders, 2 * rank // holders, inputs // groups)
     return pl.pallas_call(
         functools.partial(grads_kernel, holders),
-        out_shape=jax.ShapeDtypeStruct(slabs, jnp.float32),
+        out_shape=jax.ShapeDtypeStruct(slabs, jnp.bfloat16),
         in_specs=[pl.BlockSpec(memory_space=pltpu.SMEM)] + [vmem] * 4,
         out_specs=vmem,
         name="grads",
@@ -117,68 +118,71 @@
     return jnp.where(jnp.concatenate(values, 0) < 0, SIGN(-1), SIGN(1))
 
 
-def signs_kernel(
-    rows, columns, first_tile, salt_ref, after_ref, first_ref, second_ref, out_ref, one_ref, two_ref
-):
+def signs_kernel(rows, columns, salt_ref, after_ref, out_ref):
     del after_ref
     salt = salt_ref[0]
-    lanes = lane_terms(salt, pl.program_id(0) + first_tile)
+    lanes = lane_terms(salt, pl.program_id(0) + FEAT // TILE - EARLY)
     heights = row_heights(salt, rows)
     depth = 16 * rows
-
-    @pl.when(pl.program_id(0) == 0)
-    def _():
-        stride = first_ref.shape[0] // rows
-        for part in range(columns // 128):
-            here = pl.ds(position()[0] * (columns // 128) + part, rows, stride=stride)
-            one_ref[:, part * 128 : part * 128 + 128] = first_ref[here, :]
-            two_ref[:, part * 128 : part * 128 + 128] = second_ref[here, :]
+    blocks = out_ref.shape[1] // depth
+    first = pl.program_id(1) * blocks
 
     def store(block, _):
         here = pl.ds(pl.multiple_of(block * depth, depth), depth)
-        out_ref[0, here, :] = block_signs(salt, columns, lanes, heights, block)
+        out_ref[0, here, :] = block_signs(salt, columns, lanes, heights, first + block)
         return 0
 
-    lax.fori_loop(0, columns // 16, store, 0, unroll=2)
-
-
-def early_signs(salt, rows, columns, after, first, second):
-    whole = pl.BlockSpec((first.size // 128, 128), lambda t, i: (0, 0))
-    share = pl.BlockSpec((rows, columns), lambda t, i: (0, 0))
-    moment = jax.ShapeDtypeStruct((rows, columns), jnp.float32)
+    lax.fori_loop(0, blocks, store, 0, unroll=2)
+
+
+def early_signs(salt, rows, columns, after):
+    size = rows * columns
     return pl.pallas_call(
-        functools.partial(signs_kernel, rows, columns, FEAT // TILE - EARLY),
-        out_shape=(
-            jax.ShapeDtypeStruct((EARLY, rows * columns, TILE), SIGN),
-            moment,
-            moment,
-        ),
+        functools.partial(signs_kernel, rows, columns),
+        out_shape=jax.ShapeDtypeStruct((EARLY, size, TILE), SIGN),
         grid_spec=pltpu.PrefetchScalarGridSpec(
             num_scalar_prefetch=1,
-            grid=(EARLY,),
-            in_specs=[pl.BlockSpec(memory_space=pl.ANY), whole, whole],
-            out_specs=(
-                pl.BlockSpec((1, rows * columns, TILE), lambda t, i: (t, 0, 0)),
-                share,
-                share,
-            ),
+            grid=(EARLY, 2),
+            in_specs=[pl.BlockSpec(memory_space=pl.ANY)],
+            out_specs=pl.BlockSpec((1, size // 2, TILE), lambda t, h, i: (t, h, 0)),
         ),
         cost_estimate=pl.CostEstimate(
-            flops=EARLY * rows * columns * TILE * 256, bytes_accessed=0, transcendentals=0
+            flops=EARLY * size * TILE * 256, bytes_accessed=0, transcendentals=0
         ),
         name="early_signs",
-    )(salt, after, first.reshape(-1, 128), second.reshape(-1, 128))
-
-
-def regroup(updates_ref, grouped_ref, staged_ref, rows, columns):
-    devices = grouped_ref.shape[0]
+    )(salt, after)
+
+
+def adam_scale(grads, first, second):
+    moment_one = 0.9 * first + 0.1 * grads
+    moment_two = 0.999 * second + 0.001 * grads * grads
+    return moment_one / (jnp.sqrt(moment_two) + 1e-08)
+
+
+def keep(updates, grouped_ref, start):
+    devices, size = updates.shape
+    high = updates.astype(jnp.bfloat16)
+    grouped_ref[:devices, start : start + size] = high
+    low = updates - high.astype(jnp.float32)
+    grouped_ref[devices:, start : start + size] = low.astype(jnp.bfloat16)
+
+
+def regroup(rows, grads_ref, first_ref, second_ref, grouped_ref, staged_ref):
+    columns = grads_ref.shape[1]
+    devices = grads_ref.shape[0] // rows
+    stride = first_ref.shape[0] // rows
     lane = lax.broadcasted_iota(I32, (devices, 128), 1)
     for part in range(columns // 128):
-        staged_ref[...] = updates_ref[:, part * 128 : part * 128 + 128]
+        lanes = slice(part * 128, part * 128 + 128)
+        share = pl.ds(position()[0] * (columns // 128) + part, rows, stride=stride)
+        first, second = first_ref[share, :], second_ref[share, :]
+        for device in range(devices):
+            here = slice(device * rows, (device + 1) * rows)
+            grads = grads_ref[here, lanes].astype(jnp.float32)
+            staged_ref[here, :] = adam_scale(grads, first, second)
         for half in range(rows // 8):
             pieces = [
-                staged_ref[pl.ds(half * 8 + k, devices, stride=rows), :]
-                for k in range(8)
+                staged_ref[pl.ds(half * 8 + k, devices, stride=rows), :] for k in range(8)
             ]
             for step in (4, 2, 1):
                 upper = ((lane // 16) & step) != 0
@@ -189,8 +193,7 @@
                     pieces[k] = jnp.where(upper, pltpu.roll(b, 16 * step, 1), a)
                     pieces[k + step] = jnp.where(upper, b, pltpu.roll(a, 128 - 16 * step, 1))
             for c in range(8):
-                start = ((part * 8 + c) * rows + half * 8) * 16
-                grouped_ref[:, start : start + 128] = pieces[c].astype(jnp.bfloat16)
+                keep(pieces[c], grouped_ref, ((part * 8 + c) * rows + half * 8) * 16)
 
 
 def project_kernel(
@@ -198,50 +201,52 @@
     columns,
     scale,
     salt_ref,
-    updates_ref,
     early_ref,
-    out_ref,
-    grouped_ref,
-    staged_ref,
-    partial_ref,
-    signs_ref,
-    sems,
+    grads_ref,
+    *refs,
 ):
+    out_ref, grouped_ref, staged_ref, partial_ref, signs_ref, sems = refs[-6:]
     devices = out_ref.shape[0]
     late = FEAT // TILE - EARLY
 
     def fetch(index):
         return pltpu.make_async_copy(early_ref.at[index], signs_ref.at[index], sems.at[index])
+
+    for index in range(min(EARLY, AHEAD)):
+        fetch(index).start()
 
     def product(start, signs):
         updates = grouped_ref[:, start : start + signs.shape[0]]
         return jnp.dot(updates, signs, preferred_element_type=jnp.float32)
 
     def finish(tile, total):
-        total = total * scale
+        total = (total[:devices] + total[devices:]) * scale
         for part in range(TILE // 128):
             start = (tile * (TILE // 128) + part) * devices
             partial_ref[start : start + devices, :] = total[:, part * 128 : part * 128 + 128]
 
-    for index in range(EARLY):
-        fetch(index).start()
-    if staged_ref.shape[0] > 8:
-        regroup(updates_ref, grouped_ref, staged_ref, rows, columns)
+    if len(refs) > 6:
+        regroup(rows, grads_ref, *refs[:2], grouped_ref, staged_ref)
     else:
-        grouped_ref[...] = updates_ref[...].astype(jnp.bfloat16)
+        keep(grads_ref[...], grouped_ref, 0)
 
     salt = salt_ref[0]
     heights = row_heights(salt, rows)
     done = 0
     for tile in range(late):
-        ready = EARLY * tile // max(late - 1, 1)
-        for index in range(done, ready):
+        ready = EARLY if tile == late - 1 else min(EARLY, AHEAD * tile)
+        for index in range(max(done, AHEAD), ready):
             fetch(index).wait()
         lanes = lane_terms(salt, tile)
         totals = [0.0] * (1 + ready - done)
         blocks = columns // 16
         group = math.gcd(blocks, GROUP)
         for block in range(0, blocks, group):
+            if tile == 0 and block == blocks // 2:
+                for index in range(min(EARLY, AHEAD)):
+                    fetch(index).wait()
+                for index in range(AHEAD, EARLY):
+                    fetch(index).start()
             start, size = block * rows * 16, group * rows * 16
             for index in range(done, ready):
                 stored = signs_ref[index, start : start + size, :]
@@ -262,33 +267,40 @@
         ].astype(jnp.bfloat16)
 
 
-def project(salt, updates, early, scale):
-    m, rows, columns = updates.shape
-    if rows % 8 == 0 and columns % 128 == 0:
-        flat = updates.reshape(m * rows, columns)
-        staged = m * rows
+def project(salt, grads, first, second, early, scale):
+    m, rows, columns = grads.shape
+    vmem = pl.BlockSpec(memory_space=pltpu.VMEM)
+    if rows % 16 == 0 and columns % 128 == 0:
+        first, second = first.reshape(-1, 128), second.reshape(-1, 128)
+        operands = (grads.reshape(m * rows, columns), first, second)
     else:
-        flat = updates.reshape(m, rows, columns // 16, 16).transpose(0, 2, 1, 3)
-        flat = flat.reshape(m, rows * columns)
-        staged = 8
+
+        def share(moment):
+            start = lax.axis_index("wide") * columns
+            return lax.dynamic_slice_in_dim(moment.reshape(rows, -1), start, columns, 1)
+
+        flat = adam_scale(grads.astype(jnp.float32), share(first)[None], share(second)[None])
+        flat = flat.reshape(m, rows, columns // 16, 16).transpose(0, 2, 1, 3)
+        operands = (flat.reshape(m, rows * columns),)
     return pl.pallas_call(
         functools.partial(project_kernel, rows, columns, scale),
         out_shape=jax.ShapeDtypeStruct((m, FEAT // 128, 128), jnp.bfloat16),
         in_specs=[
             pl.BlockSpec(memory_space=pltpu.SMEM),
-            pl.BlockSpec(memory_space=pltpu.VMEM),
             pl.BlockSpec(memory_space=pl.ANY),
-        ],
-        out_specs=pl.BlockSpec(memory_space=pltpu.VMEM),
+        ]
+        + [vmem] * len(operands),
+        out_specs=vmem,
         scratch_shapes=[
-            pltpu.VMEM((m, rows * columns), jnp.bfloat16),
-            pltpu.VMEM((staged, 128), jnp.float32),
+            pltpu.VMEM((2 * m, rows * columns), jnp.bfloat16),
+            pltpu.VMEM((m * rows, 128), jnp.float32),
             pltpu.VMEM((FEAT // 128 * m, 128), jnp.float32),
             pltpu.VMEM((EARLY, rows * columns, TILE), SIGN),
             pltpu.SemaphoreType.DMA((EARLY,)),
         ],
+        compiler_params=pltpu.CompilerParams(vmem_limit_bytes=44 << 20),
         name="project",
-    )(salt, flat, early)
+    )(salt, early, *operands)
 
 
 def body(
@@ -307,21 +319,12 @@
     rank_rows = 2 * rank
     rows, columns = rank_rows // holders, inputs // groups
     params = rank_rows * inputs
-    bound = acts.shape[1] * inputs * 6 * 0.125 * 0.5
-    scale = 2.0 ** -max(0, math.ceil(math.log2(bound / 60000)))
-
     slabs = sequence_grads(groups, holders, acts, cotangent, down_matrix, up_matrix, lengths)
-    sent = (slabs * scale).astype(jnp.float16)
-    early, first, second = early_signs(
-        sign_hash_salt, rows, columns, slabs, adam_first_moment, adam_second_moment
+    early = early_signs(sign_hash_salt, rows, columns, slabs)
+    grads = lax.all_to_all(slabs, AXES, 0, 0, tiled=True)
+    partial = project(
+        sign_hash_salt, grads, adam_first_moment, adam_second_moment, early, params**-0.5
     )
-    grads = lax.all_to_all(sent, AXES, 0, 0, tiled=True).astype(jnp.float32) * (1 / scale)
-
-    moment_one = 0.9 * first[None] + 0.1 * grads
-    moment_two = 0.999 * second[None] + 0.001 * grads * grads
-    updates = moment_one / (jnp.sqrt(moment_two) + 1e-08)
-
-    partial = project(sign_hash_salt, updates, early, params**-0.5)
     parts = lax.all_to_all(partial, AXES, 0, 0, tiled=True)
     return jnp.sum(parts.astype(jnp.float32), axis=0).reshape(1, FEAT)
 

time: 65.6 us -> 58.3 us (0.89)
  other arithmetic: 5.17 us -> 0.65 us
  Pallas kernels: 34.9 us -> 32.4 us
    convert_element_type x1 -> x0, other arithmetic: 2.18 us -> none  [body(): sent = (slabs * scale).astype(jnp.float16)]
    div x1 -> x0, other arithmetic: 1.55 us -> none  [body(): updates = moment_one / (jnp.sqrt(moment_two) + 1e-08)]
    pallas_call x1, Pallas kernels: 16.4 us -> 14.9 us  [early_signs(): pl.pallas_call(functools.partial(signs_kernel, rows, columns), out_shape=...]
    pallas_call x1, Pallas kernels: 15.4 us -> 14.6 us  [project(): pl.pallas_call(functools.partial(project_kernel, rows, columns, scale), o...]
    mul x1 -> x0, other arithmetic: 0.78 us -> none  [body(): moment_two = 0.999 * second[None] + 0.001 * grads * grads]
  transfers between devices with their start and end apart: 1 -> 1, of which waited for: 0 -> 0; matrix products, arithmetic and copies ran while one was open for 1% -> 0% of each run, Pallas kernels for 25% -> 26%
where the time goes in v5:
time: 58.3 us; the launch traced here: 58 us
  Pallas kernels  32.4 us (56%)
  blocking collectives  16.2 us (28%)
  starting transfers between devices  7.32 us (13%)
  between operations  1.36 us (2%)
  other arithmetic  0.65 us (1%)
    all_to_all x1, blocking collectives, body(): parts = lax.all_to_all(partial, AXES, 0, 0, tiled=True)  16.2 us
    pallas_call x1, Pallas kernels, early_signs(): pl.pallas_call(functools.partial(signs_kernel, rows, columns), out_shape=...  14.9 us
    pallas_call x1, Pallas kernels, project(): pl.pallas_call(functools.partial(project_kernel, rows, columns, scale), o...  14.6 us
    all_to_all x1, starting transfers between devices, body(): grads = lax.all_to_all(slabs, AXES, 0, 0, tiled=True)  7.32 us
    pallas_call x1, Pallas kernels, sequence_grads(): pl.pallas_call(functools.partial(grads_kernel, holders), out_shape=jax.Sh...  2.87 us
  transfers between devices with their start and end apart: 1, of which 0 were waited for; matrix products, arithmetic and copies ran while one was open for 0% of the time, Pallas kernels for 26%

profile of v5, /device:TPU:0, one launch (start us, length us, event | category | flops | bytes accessed | tf_op | source)
XLA Modules:
  0.0 58.0 jit_solution(1272484575444657090)
XLA Ops:
  0.0 0.0 copy-start.1
  0.0 0.0 copy-start
  0.7 2.9 %grads.1.after_ref = bf16[32,16,512]{2,1,0:T(8,128)(2,1)} custom-call(s32[1]{0:T(128)S(6)} %copy.9.length_ref, bf16[128,2048]{1,0:T(8,128)(2,1)} %bitcast.10, bf16[128,2048]{1,0:T(8,128)(2,1)} %bitcast.11, bf16[64,2048]{1,0:T(8,128)(2,1)} %down_ref.1, bf16[64,2048]{1,0:T(8,128)(2,1)} %bitcast.12), custom_call_target="tpu_custom_call" | custom-call | tf_op jit(solution)/shard_map/grads/pallas_call | solution.py:57
  3.6 7.3 %all-to-all-start = ((bf16[32,16,512]{2,1,0:T(8,128)(2,1)}), bf16[32,16,512]{2,1,0:T(8,128)(2,1)S(1)}, u32[]{:S(2)}, u32[]{:S(2)}) async-start(bf16[32,16,512]{2,1,0:T(8,128)(2,1)} %grads.1.after_ref), calls=%async_computation | async-start | bytes 1048576 | tf_op jit(solution)/shard_map/all_to_all | solution.py:324
  11.5 14.9 %early_signs.1.early_ref = f8e4m3fn[5,8192,512]{2,1,0:T(32,128)(4,1)} custom-call(s32[1]{0:T(128)S(6)} %copy.10.salt_ref, bf16[32,16,512]{2,1,0:T(8,128)(2,1)} %grads.1.after_ref), custom_call_target="tpu_custom_call" | custom-call | flops 5368709120 | tf_op jit(solution)/shard_map/early_signs/pallas_call | solution.py:140
  26.5 0.0 all-to-all-done
  26.5 0.0 copy-done.1
  26.5 0.0 copy-done
  26.5 14.6 %project.1 = bf16[32,32,128]{2,1,0:T(8,128)(2,1)S(1)} custom-call(s32[1]{0:T(128)S(6)} %copy.10.salt_ref, f8e4m3fn[5,8192,512]{2,1,0:T(32,128)(4,1)} %early_signs.1.early_ref, bf16[512,512]{1,0:T(8,128)(2,1)S(1)} %bitcast.7, f32[256,128]{1,0:T(8,128)S(1)} %bitcast.8, f32[256,128]{1,0:T(8,128)S(1)} %bitcast.9), custom_call_target="tpu_custom_call" | custom-call | tf_op jit(solution)/shard_map/project/pallas_call | solution.py:285
  41.1 16.2 %all_to_all.10 = bf16[32,32,128]{2,1,0:T(8,128)(2,1)S(1)} all-to-all(bf16[32,32,128]{2,1,0:T(8,128)(2,1)S(1)} %project.1), channel_id=1, replica_groups=mesh['wide'=4,'narrow'=8] {'wide','narrow'}, dimensions={0} | all-to-all | bytes 524288 | tf_op jit(solution)/shard_map/all_to_all | solution.py:328
  57.4 0.7 %convert_reduce_fusion = f32[32,128]{1,0:T(8,128)} fusion(bf16[32,32,128]{2,1,0:T(8,128)(2,1)S(1)} %all_to_all.10), kind=kLoop, calls=%fused_computation | loop fusion | flops 258048 | bytes 278528 | tf_op jit(solution)/shard_map/reduce_sum | solution.py:329
Async XLA Ops:
  0.0 26.5 %copy-start.1 = (f32[32768]{0:T(1024)S(1)}, f32[32768]{0:T(1024)}, u32[]{:S(2)}) copy-start(f32[32768]{0:T(1024)} %param.13) | copy-start | bytes 393220
  0.0 26.5 %copy-start = (f32[32768]{0:T(1024)S(1)}, f32[32768]{0:T(1024)}, u32[]{:S(2)}) copy-start(f32[32768]{0:T(1024)} %param.12) | copy-start | bytes 393220
  3.6 22.9 %all-to-all-start = ((bf16[32,16,512]{2,1,0:T(8,128)(2,1)}), bf16[32,16,512]{2,1,0:T(8,128)(2,1)S(1)}, u32[]{:S(2)}, u32[]{:S(2)}) async-start(bf16[32,16,512]{2,1,0:T(8,128)(2,1)} %grads.1.after_ref), calls=%async_computation | async-start | bytes 1048576 | tf_op jit(solution)/shard_map/all_to_all | solution.py:324

commit v6 on v5

--- a/solution.py
+++ b/solution.py
@@ -17,7 +17,9 @@
 LOW = (1 << COLUMN_BITS) - 1
 TILE = 512
 GROUP = 2
-AHEAD = 2
+SPLIT = 8
+FIRST, EACH = 5, 9
+AHEAD = 3
 EARLY = 5
 I16 = jnp.int16
 I32 = jnp.int32
@@ -210,10 +212,24 @@
     late = FEAT // TILE - EARLY
 
     def fetch(index):
-        return pltpu.make_async_copy(early_ref.at[index], signs_ref.at[index], sems.at[index])
-
-    for index in range(min(EARLY, AHEAD)):
-        fetch(index).start()
+        size = early_ref.shape[1] // SPLIT
+        pieces = [(index, pl.ds(piece * size, size)) for piece in range(SPLIT)]
+        return [
+            pltpu.make_async_copy(early_ref.at[at], signs_ref.at[at], sems.at[index, piece])
+            for piece, at in enumerate(pieces)
+        ]
+
+    def start(indices):
+        for index in indices:
+            for copy in fetch(index):
+                copy.start()
+
+    def wait(indices):
+        for index in indices:
+            for copy in fetch(index):
+                copy.wait()
+
+    start(range(min(EARLY, AHEAD)))
 
     def product(start, signs):
         updates = grouped_ref[:, start : start + signs.shape[0]]
@@ -232,34 +248,49 @@
 
     salt = salt_ref[0]
     heights = row_heights(salt, rows)
-    done = 0
-    for tile in range(late):
-        ready = EARLY if tile == late - 1 else min(EARLY, AHEAD * tile)
-        for index in range(max(done, AHEAD), ready):
-            fetch(index).wait()
-        lanes = lane_terms(salt, tile)
-        totals = [0.0] * (1 + ready - done)
-        blocks = columns // 16
-        group = math.gcd(blocks, GROUP)
-        for block in range(0, blocks, group):
-            if tile == 0 and block == blocks // 2:
-                for index in range(min(EARLY, AHEAD)):
-                    fetch(index).wait()
-                for index in range(AHEAD, EARLY):
-                    fetch(index).start()
-            start, size = block * rows * 16, group * rows * 16
-            for index in range(done, ready):
-                stored = signs_ref[index, start : start + size, :]
-                totals[1 + index - done] += product(start, stored)
+    batches = [range(at, min(EARLY, at + AHEAD)) for at in range(0, EARLY, AHEAD)]
+    fetched, ready = 0, []
+    blocks = columns // 16
+    depth = rows * 16
+    half = max(blocks // 2, 1)
+    group = math.gcd(half, GROUP)
+
+    def take():
+        nonlocal fetched
+        wait(batches[fetched])
+        ready.extend(batches[fetched])
+        fetched += 1
+        if fetched < len(batches):
+            start(batches[fetched])
+
+    for step in range(late * (blocks // half)):
+        if fetched < len(batches) and step >= FIRST + fetched * EACH:
+            take()
+        tile, first = divmod(step * half, blocks)
+        stored = ready.pop(0) if ready else None
+        if first == 0:
+            lanes = lane_terms(salt, tile)
+            made = 0.0
+        other = 0.0
+        for block in range(first, first + half, group):
+            if stored is not None:
+                share = signs_ref.shape[1] // (half // group)
+                begin = (block - first) // group * share
+                other += product(begin, signs_ref[stored, begin : begin + share, :])
             signs = [
                 block_signs(salt, columns, lanes, heights, block + member)
                 for member in range(group)
             ]
-            totals[0] += product(start, jnp.concatenate(signs, 0))
-        finish(tile, totals[0])
-        for index in range(done, ready):
-            finish(late + index, totals[1 + index - done])
-        done = ready
+            made += product(block * depth, jnp.concatenate(signs, 0))
+        if first + half == blocks:
+            finish(tile, made)
+        if stored is not None:
+            finish(late + stored, other)
+    while ready or fetched < len(batches):
+        if not ready:
+            take()
+        stored = ready.pop(0)
+        finish(late + stored, product(0, signs_ref[stored]))
 
     for device in range(devices):
         out_ref[device] = partial_ref[
@@ -296,7 +327,7 @@
             pltpu.VMEM((m * rows, 128), jnp.float32),
             pltpu.VMEM((FEAT // 128 * m, 128), jnp.float32),
             pltpu.VMEM((EARLY, rows * columns, TILE), SIGN),
-            pltpu.SemaphoreType.DMA((EARLY,)),
+            pltpu.SemaphoreType.DMA((EARLY, SPLIT)),
         ],
         compiler_params=pltpu.CompilerParams(vmem_limit_bytes=44 << 20),
         name="project",

time: 58.3 us -> 57.1 us (0.979)
  Pallas kernels: 32.4 us -> 31.3 us
    pallas_call x1, Pallas kernels: 14.6 us -> 13.5 us  [project(): pl.pallas_call(functools.partial(project_kernel, rows, columns, scale), o...]
where the time goes in v6:
time: 57.1 us; the launch traced here: 56.8 us
  Pallas kernels  31.3 us (55%)
  blocking collectives  16.2 us (28%)
  starting transfers between devices  7.32 us (13%)
  between operations  1.36 us (2%)
  other arithmetic  0.65 us (1%)
    all_to_all x1, blocking collectives, body(): parts = lax.all_to_all(partial, AXES, 0, 0, tiled=True)  16.2 us
    pallas_call x1, Pallas kernels, early_signs(): pl.pallas_call(functools.partial(signs_kernel, rows, columns), out_shape=...  14.9 us
    pallas_call x1, Pallas kernels, project(): pl.pallas_call(functools.partial(project_kernel, rows, columns, scale), o...  13.5 us
    all_to_all x1, starting transfers between devices, body(): grads = lax.all_to_all(slabs, AXES, 0, 0, tiled=True)  7.32 us
    pallas_call x1, Pallas kernels, sequence_grads(): pl.pallas_call(functools.partial(grads_kernel, holders), out_shape=jax.Sh...  2.87 us
  transfers between devices with their start and end apart: 1, of which 0 were waited for; matrix products, arithmetic and copies ran while one was open for 0% of the time, Pallas kernels for 26%

profile of v6, /device:TPU:0, one launch (start us, length us, event | category | flops | bytes accessed | tf_op | source)
XLA Modules:
  0.0 56.8 jit_solution(5277958450888726468)
XLA Ops:
  0.0 0.0 copy-start.1
  0.0 0.0 copy-start
  0.7 2.9 %grads.1.after_ref = bf16[32,16,512]{2,1,0:T(8,128)(2,1)} custom-call(s32[1]{0:T(128)S(6)} %copy.9.length_ref, bf16[128,2048]{1,0:T(8,128)(2,1)} %bitcast.10, bf16[128,2048]{1,0:T(8,128)(2,1)} %bitcast.11, bf16[64,2048]{1,0:T(8,128)(2,1)} %down_ref.1, bf16[64,2048]{1,0:T(8,128)(2,1)} %bitcast.12), custom_call_target="tpu_custom_call" | custom-call | tf_op jit(solution)/shard_map/grads/pallas_call | solution.py:59
  3.6 7.3 %all-to-all-start = ((bf16[32,16,512]{2,1,0:T(8,128)(2,1)}), bf16[32,16,512]{2,1,0:T(8,128)(2,1)S(1)}, u32[]{:S(2)}, u32[]{:S(2)}) async-start(bf16[32,16,512]{2,1,0:T(8,128)(2,1)} %grads.1.after_ref), calls=%async_computation | async-start | bytes 1048576 | tf_op jit(solution)/shard_map/all_to_all | solution.py:355
  11.5 14.9 %early_signs.1.early_ref = f8e4m3fn[5,8192,512]{2,1,0:T(32,128)(4,1)} custom-call(s32[1]{0:T(128)S(6)} %copy.10.salt_ref, bf16[32,16,512]{2,1,0:T(8,128)(2,1)} %grads.1.after_ref), custom_call_target="tpu_custom_call" | custom-call | flops 5368709120 | tf_op jit(solution)/shard_map/early_signs/pallas_call | solution.py:142
  26.5 0.0 all-to-all-done
  26.5 0.0 copy-done.1
  26.5 0.0 copy-done
  26.5 13.5 %project.1 = bf16[32,32,128]{2,1,0:T(8,128)(2,1)S(1)} custom-call(s32[1]{0:T(128)S(6)} %copy.10.salt_ref, f8e4m3fn[5,8192,512]{2,1,0:T(32,128)(4,1)} %early_signs.1.early_ref, bf16[512,512]{1,0:T(8,128)(2,1)S(1)} %bitcast.7, f32[256,128]{1,0:T(8,128)S(1)} %bitcast.8, f32[256,128]{1,0:T(8,128)S(1)} %bitcast.9), custom_call_target="tpu_custom_call" | custom-call | tf_op jit(solution)/shard_map/project/pallas_call | solution.py:316
  40.0 16.2 %all_to_all.10 = bf16[32,32,128]{2,1,0:T(8,128)(2,1)S(1)} all-to-all(bf16[32,32,128]{2,1,0:T(8,128)(2,1)S(1)} %project.1), channel_id=1, replica_groups=mesh['wide'=4,'narrow'=8] {'wide','narrow'}, dimensions={0} | all-to-all | bytes 524288 | tf_op jit(solution)/shard_map/all_to_all | solution.py:359
  56.2 0.7 %convert_reduce_fusion = f32[32,128]{1,0:T(8,128)} fusion(bf16[32,32,128]{2,1,0:T(8,128)(2,1)S(1)} %all_to_all.10), kind=kLoop, calls=%fused_computation | loop fusion | flops 258048 | bytes 278528 | tf_op jit(solution)/shard_map/reduce_sum | solution.py:360
Async XLA Ops:
  0.0 26.5 %copy-start.1 = (f32[32768]{0:T(1024)S(1)}, f32[32768]{0:T(1024)}, u32[]{:S(2)}) copy-start(f32[32768]{0:T(1024)} %param.13) | copy-start | bytes 393220
  0.0 26.5 %copy-start = (f32[32768]{0:T(1024)S(1)}, f32[32768]{0:T(1024)}, u32[]{:S(2)}) copy-start(f32[32768]{0:T(1024)} %param.12) | copy-start | bytes 393220
  3.6 22.9 %all-to-all-start = ((bf16[32,16,512]{2,1,0:T(8,128)(2,1)}), bf16[32,16,512]{2,1,0:T(8,128)(2,1)S(1)}, u32[]{:S(2)}, u32[]{:S(2)}) async-start(bf16[32,16,512]{2,1,0:T(8,128)(2,1)} %grads.1.after_ref), calls=%async_computation | async-start | bytes 1048576 | tf_op jit(solution)/shard_map/all_to_all | solution.py:355

commit v7 on v6

--- a/solution.py
+++ b/solution.py
@@ -19,6 +19,7 @@
 GROUP = 2
 SPLIT = 8
 FIRST, EACH = 5, 9
+NEXT = 3
 AHEAD = 3
 EARLY = 5
 I16 = jnp.int16
@@ -249,21 +250,28 @@
     salt = salt_ref[0]
     heights = row_heights(salt, rows)
     batches = [range(at, min(EARLY, at + AHEAD)) for at in range(0, EARLY, AHEAD)]
-    fetched, ready = 0, []
+    fetched, started, ready = 0, 1, []
     blocks = columns // 16
     depth = rows * 16
     half = max(blocks // 2, 1)
     group = math.gcd(half, GROUP)
 
+    def begin_next(count):
+        nonlocal started
+        while started < min(count, len(batches)):
+            start(batches[started])
+            started += 1
+
     def take():
         nonlocal fetched
+        begin_next(fetched + 1)
         wait(batches[fetched])
         ready.extend(batches[fetched])
         fetched += 1
-        if fetched < len(batches):
-            start(batches[fetched])
 
     for step in range(late * (blocks // half)):
+        if step == NEXT:
+            begin_next(2)
         if fetched < len(batches) and step >= FIRST + fetched * EACH:
             take()
         tile, first = divmod(step * half, blocks)

time: 57.1 us -> 56.5 us (0.989)
  Pallas kernels: 31.3 us -> 30.6 us
    pallas_call x1, Pallas kernels: 13.5 us -> 12.8 us  [project(): pl.pallas_call(functools.partial(project_kernel, rows, columns, scale), o...]
  transfers between devices with their start and end apart: 1 -> 1, of which waited for: 0 -> 0; matrix products, arithmetic and copies ran while one was open for 0% -> 0% of each run, Pallas kernels for 26% -> 27%
where the time goes in v7:
time: 56.5 us; the launch traced here: 56.2 us
  Pallas kernels  30.6 us (54%)
  blocking collectives  16.2 us (29%)
  starting transfers between devices  7.32 us (13%)
  between operations  1.36 us (2%)
  other arithmetic  0.65 us (1%)
    all_to_all x1, blocking collectives, body(): parts = lax.all_to_all(partial, AXES, 0, 0, tiled=True)  16.2 us
    pallas_call x1, Pallas kernels, early_signs(): pl.pallas_call(functools.partial(signs_kernel, rows, columns), out_shape=...  14.9 us
    pallas_call x1, Pallas kernels, project(): pl.pallas_call(functools.partial(project_kernel, rows, columns, scale), o...  12.8 us
    all_to_all x1, starting transfers between devices, body(): grads = lax.all_to_all(slabs, AXES, 0, 0, tiled=True)  7.32 us
    pallas_call x1, Pallas kernels, sequence_grads(): pl.pallas_call(functools.partial(grads_kernel, holders), out_shape=jax.Sh...  2.87 us
  transfers between devices with their start and end apart: 1, of which 0 were waited for; matrix products, arithmetic and copies ran while one was open for 0% of the time, Pallas kernels for 27%

profile of v7, /device:TPU:0, one launch (start us, length us, event | category | flops | bytes accessed | tf_op | source)
XLA Modules:
  0.0 56.2 jit_solution(12889393427914815829)
XLA Ops:
  0.0 0.0 copy-start.1
  0.0 0.0 copy-start
  0.7 2.9 %grads.1.after_ref = bf16[32,16,512]{2,1,0:T(8,128)(2,1)} custom-call(s32[1]{0:T(128)S(6)} %copy.9.length_ref, bf16[128,2048]{1,0:T(8,128)(2,1)} %bitcast.10, bf16[128,2048]{1,0:T(8,128)(2,1)} %bitcast.11, bf16[64,2048]{1,0:T(8,128)(2,1)} %down_ref.1, bf16[64,2048]{1,0:T(8,128)(2,1)} %bitcast.12), custom_call_target="tpu_custom_call" | custom-call | tf_op jit(solution)/shard_map/grads/pallas_call | solution.py:60
  3.6 7.3 %all-to-all-start = ((bf16[32,16,512]{2,1,0:T(8,128)(2,1)}), bf16[32,16,512]{2,1,0:T(8,128)(2,1)S(1)}, u32[]{:S(2)}, u32[]{:S(2)}) async-start(bf16[32,16,512]{2,1,0:T(8,128)(2,1)} %grads.1.after_ref), calls=%async_computation | async-start | bytes 1048576 | tf_op jit(solution)/shard_map/all_to_all | solution.py:363
  11.5 14.9 %early_signs.1.early_ref = f8e4m3fn[5,8192,512]{2,1,0:T(32,128)(4,1)} custom-call(s32[1]{0:T(128)S(6)} %copy.10.salt_ref, bf16[32,16,512]{2,1,0:T(8,128)(2,1)} %grads.1.after_ref), custom_call_target="tpu_custom_call" | custom-call | flops 5368709120 | tf_op jit(solution)/shard_map/early_signs/pallas_call | solution.py:143
  26.5 0.0 all-to-all-done
  26.5 0.0 copy-done.1
  26.5 0.0 copy-done
  26.5 12.8 %project.1 = bf16[32,32,128]{2,1,0:T(8,128)(2,1)S(1)} custom-call(s32[1]{0:T(128)S(6)} %copy.10.salt_ref, f8e4m3fn[5,8192,512]{2,1,0:T(32,128)(4,1)} %early_signs.1.early_ref, bf16[512,512]{1,0:T(8,128)(2,1)S(1)} %bitcast.7, f32[256,128]{1,0:T(8,128)S(1)} %bitcast.8, f32[256,128]{1,0:T(8,128)S(1)} %bitcast.9), custom_call_target="tpu_custom_call" | custom-call | tf_op jit(solution)/shard_map/project/pallas_call | solution.py:324
  39.3 16.2 %all_to_all.10 = bf16[32,32,128]{2,1,0:T(8,128)(2,1)S(1)} all-to-all(bf16[32,32,128]{2,1,0:T(8,128)(2,1)S(1)} %project.1), channel_id=1, replica_groups=mesh['wide'=4,'narrow'=8] {'wide','narrow'}, dimensions={0} | all-to-all | bytes 524288 | tf_op jit(solution)/shard_map/all_to_all | solution.py:367
  55.5 0.7 %convert_reduce_fusion = f32[32,128]{1,0:T(8,128)} fusion(bf16[32,32,128]{2,1,0:T(8,128)(2,1)S(1)} %all_to_all.10), kind=kLoop, calls=%fused_computation | loop fusion | flops 258048 | bytes 278528 | tf_op jit(solution)/shard_map/reduce_sum | solution.py:368
Async XLA Ops:
  0.0 26.5 %copy-start.1 = (f32[32768]{0:T(1024)S(1)}, f32[32768]{0:T(1024)}, u32[]{:S(2)}) copy-start(f32[32768]{0:T(1024)} %param.13) | copy-start | bytes 393220
  0.0 26.5 %copy-start = (f32[32768]{0:T(1024)S(1)}, f32[32768]{0:T(1024)}, u32[]{:S(2)}) copy-start(f32[32768]{0:T(1024)} %param.12) | copy-start | bytes 393220
  3.6 22.9 %all-to-all-start = ((bf16[32,16,512]{2,1,0:T(8,128)(2,1)}), bf16[32,16,512]{2,1,0:T(8,128)(2,1)S(1)}, u32[]{:S(2)}, u32[]{:S(2)}) async-start(bf16[32,16,512]{2,1,0:T(8,128)(2,1)} %grads.1.after_ref), calls=%async_computation | async-start | bytes 1048576 | tf_op jit(solution)/shard_map/all_to_all | solution.py:363

commit v8 on v7

--- a/solution.py
+++ b/solution.py
@@ -145,9 +145,9 @@
         out_shape=jax.ShapeDtypeStruct((EARLY, size, TILE), SIGN),
         grid_spec=pltpu.PrefetchScalarGridSpec(
             num_scalar_prefetch=1,
-            grid=(EARLY, 2),
+            grid=(EARLY, 4),
             in_specs=[pl.BlockSpec(memory_space=pl.ANY)],
-            out_specs=pl.BlockSpec((1, size // 2, TILE), lambda t, h, i: (t, h, 0)),
+            out_specs=pl.BlockSpec((1, size // 4, TILE), lambda t, h, i: (t, h, 0)),
         ),
         cost_estimate=pl.CostEstimate(
             flops=EARLY * size * TILE * 256, bytes_accessed=0, transcendentals=0

time: 56.5 us -> 59 us (1.044)
  Pallas kernels: 30.6 us -> 33.2 us
    pallas_call x1, Pallas kernels: 14.9 us -> 17.5 us  [early_signs(): pl.pallas_call(functools.partial(signs_kernel, rows, columns), out_shape=...]
  transfers between devices with their start and end apart: 1 -> 1, of which waited for: 0 -> 0; matrix products, arithmetic and copies ran while one was open for 0% -> 0% of each run, Pallas kernels for 27% -> 30%
where the time goes in v8:
time: 59 us; the launch traced here: 58.7 us
  Pallas kernels  33.2 us (56%)
  blocking collectives  16.2 us (27%)
  starting transfers between devices  7.32 us (12%)
  between operations  1.37 us (2%)
  other arithmetic  0.65 us (1%)
    pallas_call x1, Pallas kernels, early_signs(): pl.pallas_call(functools.partial(signs_kernel, rows, columns), out_shape=...  17.5 us
    all_to_all x1, blocking collectives, body(): parts = lax.all_to_all(partial, AXES, 0, 0, tiled=True)  16.2 us
    pallas_call x1, Pallas kernels, project(): pl.pallas_call(functools.partial(project_kernel, rows, columns, scale), o...  12.8 us
    all_to_all x1, starting transfers between devices, body(): grads = lax.all_to_all(slabs, AXES, 0, 0, tiled=True)  7.32 us
    pallas_call x1, Pallas kernels, sequence_grads(): pl.pallas_call(functools.partial(grads_kernel, holders), out_shape=jax.Sh...  2.87 us
  transfers between devices with their start and end apart: 1, of which 0 were waited for; matrix products, arithmetic and copies ran while one was open for 0% of the time, Pallas kernels for 30%

profile of v8, /device:TPU:0, one launch (start us, length us, event | category | flops | bytes accessed | tf_op | source)
XLA Modules:
  0.0 58.7 jit_solution(15576068876663794677)
XLA Ops:
  0.0 0.0 copy-start.1
  0.0 0.0 copy-start
  0.7 2.9 %grads.1.after_ref = bf16[32,16,512]{2,1,0:T(8,128)(2,1)} custom-call(s32[1]{0:T(128)S(6)} %copy.9.length_ref, bf16[128,2048]{1,0:T(8,128)(2,1)} %bitcast.10, bf16[128,2048]{1,0:T(8,128)(2,1)} %bitcast.11, bf16[64,2048]{1,0:T(8,128)(2,1)} %down_ref.1, bf16[64,2048]{1,0:T(8,128)(2,1)} %bitcast.12), custom_call_target="tpu_custom_call" | custom-call | tf_op jit(solution)/shard_map/grads/pallas_call | solution.py:60
  3.6 7.3 %all-to-all-start = ((bf16[32,16,512]{2,1,0:T(8,128)(2,1)}), bf16[32,16,512]{2,1,0:T(8,128)(2,1)S(1)}, u32[]{:S(2)}, u32[]{:S(2)}) async-start(bf16[32,16,512]{2,1,0:T(8,128)(2,1)} %grads.1.after_ref), calls=%async_computation | async-start | bytes 1048576 | tf_op jit(solution)/shard_map/all_to_all | solution.py:363
  11.5 17.5 %early_signs.1.early_ref = f8e4m3fn[5,8192,512]{2,1,0:T(32,128)(4,1)} custom-call(s32[1]{0:T(128)S(6)} %copy.10.salt_ref, bf16[32,16,512]{2,1,0:T(8,128)(2,1)} %grads.1.after_ref), custom_call_target="tpu_custom_call" | custom-call | flops 5368709120 | tf_op jit(solution)/shard_map/early_signs/pallas_call | solution.py:143
  29.1 0.0 all-to-all-done
  29.1 0.0 copy-done.1
  29.1 0.0 copy-done
  29.1 12.8 %project.1 = bf16[32,32,128]{2,1,0:T(8,128)(2,1)S(1)} custom-call(s32[1]{0:T(128)S(6)} %copy.10.salt_ref, f8e4m3fn[5,8192,512]{2,1,0:T(32,128)(4,1)} %early_signs.1.early_ref, bf16[512,512]{1,0:T(8,128)(2,1)S(1)} %bitcast.7, f32[256,128]{1,0:T(8,128)S(1)} %bitcast.8, f32[256,128]{1,0:T(8,128)S(1)} %bitcast.9), custom_call_target="tpu_custom_call" | custom-call | tf_op jit(solution)/shard_map/project/pallas_call | solution.py:324
  41.9 16.2 %all_to_all.10 = bf16[32,32,128]{2,1,0:T(8,128)(2,1)S(1)} all-to-all(bf16[32,32,128]{2,1,0:T(8,128)(2,1)S(1)} %project.1), channel_id=1, replica_groups=mesh['wide'=4,'narrow'=8] {'wide','narrow'}, dimensions={0} | all-to-all | bytes 524288 | tf_op jit(solution)/shard_map/all_to_all | solution.py:367
  58.1 0.7 %convert_reduce_fusion = f32[32,128]{1,0:T(8,128)} fusion(bf16[32,32,128]{2,1,0:T(8,128)(2,1)S(1)} %all_to_all.10), kind=kLoop, calls=%fused_computation | loop fusion | flops 258048 | bytes 278528 | tf_op jit(solution)/shard_map/reduce_sum | solution.py:368
Async XLA Ops:
  0.0 29.1 %copy-start.1 = (f32[32768]{0:T(1024)S(1)}, f32[32768]{0:T(1024)}, u32[]{:S(2)}) copy-start(f32[32768]{0:T(1024)} %param.13) | copy-start | bytes 393220
  0.0 29.1 %copy-start = (f32[32768]{0:T(1024)S(1)}, f32[32768]{0:T(1024)}, u32[]{:S(2)}) copy-start(f32[32768]{0:T(1024)} %param.12) | copy-start | bytes 393220
  3.6 25.5 %all-to-all-start = ((bf16[32,16,512]{2,1,0:T(8,128)(2,1)}), bf16[32,16,512]{2,1,0:T(8,128)(2,1)S(1)}, u32[]{:S(2)}, u32[]{:S(2)}) async-start(bf16[32,16,512]{2,1,0:T(8,128)(2,1)} %grads.1.after_ref), calls=%async_computation | async-start | bytes 1048576 | tf_op jit(solution)/shard_map/all_to_all | solution.py:363
